TPU v7x, 32 devices: a whole 2x2x4 slice. The times are simulated.
32 devices in a mesh: section: 8 (over z, y), rep: 4 (over x, core).
Axes of the slice: x: 2, y: 2, z: 4, core: 2. Of those that a mesh axis runs over, the one named last changes fastest.
Arguments:
- document_token_embedding: bfloat16 [8, 128, 4096], P('rep'), may hold values from -6 to 6
- doc_lengths: int32 [8, 4], P('rep'), may hold values from 1 to 32, as said below
- docid_embed: bfloat16 [8, 32, 4096], P('rep'), may hold values from -6 to 6
- docid_targets: int32 [8, 32], P('rep'), may hold values from 0 to 16383
- enc_gain: float32 [5, 4096], replicated, may hold values from 0.1 to 1.9
- dec_gain: float32 [2, 4096], replicated, may hold values from 0.1 to 1.9
- w_enc_qkv: bfloat16 [3, 12288, 4096], P(None, 'section'), may hold values from -0.03125 to 0.03125
- w_enc_out: bfloat16 [12288, 4096], P('section'), may hold values from -0.75 to 0.75
- cross_query_key_value_weight: bfloat16 [3, 4096, 4096], P(None, 'section'), may hold values from -0.03125 to 0.03125
- w_cross_out: bfloat16 [4096, 4096], P('section'), may hold values from -0.75 to 0.75
- docid_head_weight: bfloat16 [4096, 16384], P(None, 'section'), may hold values from -0.25 to 0.25
Outputs:
- logits: bfloat16 [8, 32, 16384], P('rep', None, 'section')
- token_loss: float32 [8, 32], P('rep')
- mean_loss: float32 [], replicated
Inputs may be any that keep to these rules, and one draw needn't show every extreme that they name: `doc_lengths`: in every draw some document has exactly 32 tokens.
All inputs are finite; a program needn't handle non-finite values.
Results may differ from a plain program's by a relative error of at most 0.019.
Values may be sent and summed in bfloat16 or wider, within the bound.
A program may use at most 128 MiB of HBM per device.

v0:
```python
import functools

import jax
import jax.numpy as jnp
from jax import lax
from jax.experimental import pallas as pl
from jax.experimental.pallas import tpu as pltpu
from jax.sharding import PartitionSpec as P

HD = 64
GROUPS = 4
WTILE = 512
PARTS = 4
CHUNKS = 8
AHEAD = 2
MESH = pl.DeviceIdType.MESH


def from_partner(block, axis, distance):
    count = lax.axis_size(axis)
    route = []
    for low in range(count):
        high = low | 1 << distance
        if high != low and high < count:
            route += [(low, high), (high, low)]
    return lax.ppermute(block, axis, route)


def from_behind(block, axis, distance):
    devices = range(lax.axis_size(axis))
    route = [(i - distance, i) for i in devices if i - distance in devices]
    return lax.ppermute(block, axis, route)


def passed_along(shard, axis, by):
    size = lax.axis_size(axis)
    return lax.ppermute(shard, axis, [(i, (i + by) % size) for i in range(size)])


def norm_rows(values, gain):
    values = values.astype(jnp.float32)
    scale = lax.rsqrt(jnp.mean(values * values, axis=-1, keepdims=True) + 1e-06)
    return values * scale * gain


def attend(queries, key_rows, values, allowed):
    scores = jnp.einsum("qhe,khe->hqk", queries, key_rows, preferred_element_type=jnp.float32)
    attention_weight_rows = jnp.where(allowed[None], jnp.exp(scores), 0.0)
    probabilities = (
        attention_weight_rows / jnp.sum(attention_weight_rows, axis=-1, keepdims=True)
    ).astype(jnp.bfloat16)
    mixture = jnp.einsum("hqk,khe->qhe", probabilities, values, preferred_element_type=jnp.float32)
    return mixture.astype(jnp.bfloat16)


def live_keys(lengths, key_doc, key_place):
    owners = jnp.arange(lengths.shape[0])
    matches = (key_doc[:, None] == owners[None, :]) & (key_place[:, None] < lengths[None, :])
    return jnp.any(matches, axis=1)


def lane_gather(own_rows, lane_bits, lane_index, concat_dim):
    for bit_number in range(lane_bits):
        partner = from_partner(own_rows, "section", bit_number)
        lower_half = lane_index // (1 << bit_number) % 2 == 0
        own_rows = jnp.where(
            lower_half,
            jnp.concatenate([own_rows, partner], concat_dim),
            jnp.concatenate([partner, own_rows], concat_dim),
        )
    return own_rows


def lane_reduce(totals, lane_bits, lane_index):
    for bit_number in reversed(range(lane_bits)):
        half_rows = totals.shape[0] // 2
        lower_half = lane_index // (1 << bit_number) % 2 == 0
        kept_rows = jnp.where(lower_half, totals[:half_rows], totals[half_rows:])
        outgoing = jnp.where(lower_half, totals[half_rows:], totals[:half_rows])
        totals = kept_rows + from_partner(outgoing, "section", bit_number)
    return totals


def relay_memory(encoder_memory, group_index, lane_count):
    encoder_memory = jnp.where(group_index == 0, encoder_memory, jnp.zeros_like(encoder_memory))
    for stride in (1, 2):
        encoder_memory = encoder_memory + from_behind(
            encoder_memory, "section", stride * lane_count
        )
    return encoder_memory


def shards(
    document_token_embedding,
    doc_lengths,
    docid_embed,
    docid_targets,
    enc_gain,
    dec_gain,
    w_enc_qkv,
    w_enc_out,
    cross_query_key_value_weight,
    w_cross_out,
    docid_head_weight,
):
    lane_count = lax.axis_size("section") // GROUPS
    lane_bits = lane_count.bit_length() - 1
    section_index = lax.axis_index("section")
    group_index = section_index // lane_count
    lane_index = section_index % lane_count
    micro_count, row_count, model_width = document_token_embedding.shape
    doc_count = doc_lengths.shape[1]
    doc_span = row_count // doc_count
    block_rows = row_count // lane_count
    local_heads = w_enc_qkv.shape[1] // HD
    positions = jnp.arange(row_count)
    key_doc = positions // doc_span
    key_place = positions % doc_span
    same_doc = key_doc[:, None] == key_doc[None, :]

    def partial_update(normed, lengths):
        allowed = same_doc & live_keys(lengths, key_doc, key_place)[None, :]
        projected = jnp.einsum(
            "rd,mcd->mrc", normed, w_enc_qkv, preferred_element_type=jnp.float32
        ).astype(jnp.bfloat16)
        projected = projected.reshape(3, row_count, local_heads, HD)
        mixture = attend(projected[0], projected[1], projected[2], allowed).reshape(row_count, -1)
        return jnp.dot(mixture, w_enc_out, preferred_element_type=jnp.float32)

    def section_step(step_index, loop_state):
        handed, encoder_memory = loop_state
        micro_index = step_index - group_index
        slot_index = jnp.clip(micro_index, 0, micro_count - 1)
        lengths = lax.dynamic_index_in_dim(doc_lengths, slot_index, 0, keepdims=False)
        layer_gain = lax.dynamic_index_in_dim(enc_gain, group_index, 0, keepdims=False)
        incoming = lax.dynamic_index_in_dim(
            document_token_embedding, jnp.minimum(step_index, micro_count - 1), 0, keepdims=False
        )
        incoming = lax.dynamic_slice_in_dim(incoming, lane_index * block_rows, block_rows, 0)
        current = jnp.where(group_index == 0, incoming, handed)
        normed = lane_gather(
            norm_rows(current, layer_gain).astype(jnp.bfloat16), lane_bits, lane_index, 0
        )
        summed = lane_reduce(partial_update(normed, lengths), lane_bits, lane_index)
        result = (current.astype(jnp.float32) + summed).astype(jnp.bfloat16)
        handed = passed_along(result, "section", lane_count)
        finished_index = step_index - (GROUPS - 1)
        finished_slot = jnp.clip(finished_index, 0, micro_count - 1)
        keeping = (group_index == 0) & (finished_index >= 0) & (finished_index < micro_count)
        stored = lax.dynamic_update_index_in_dim(encoder_memory, handed, finished_slot, 0)
        encoder_memory = jnp.where(keeping, stored, encoder_memory)
        return (handed, encoder_memory)

    handed = jnp.zeros((block_rows, model_width), jnp.bfloat16)
    encoder_memory = jnp.zeros((micro_count, block_rows, model_width), jnp.bfloat16)
    handed, encoder_memory = lax.fori_loop(
        0, micro_count + GROUPS - 1, section_step, (handed, encoder_memory)
    )
    encoder_memory = norm_rows(encoder_memory, enc_gain[GROUPS]).astype(jnp.bfloat16)
    encoder_memory = relay_memory(encoder_memory, group_index, lane_count)
    encoder_memory = lane_gather(encoder_memory, lane_bits, lane_index, 1)
    decoder_rows = docid_embed.shape[1]
    docid_span = decoder_rows // doc_count
    decoder_doc = jnp.arange(decoder_rows) // docid_span
    cross_heads = cross_query_key_value_weight.shape[1] // HD
    dec_normed = norm_rows(docid_embed, dec_gain[0]).astype(jnp.bfloat16)
    queries = jnp.einsum(
        "brd,cd->brc",
        dec_normed,
        cross_query_key_value_weight[0],
        preferred_element_type=jnp.float32,
    ).astype(jnp.bfloat16)
    memory_heads = jnp.einsum(
        "pye,qve->qpyv",
        encoder_memory,
        cross_query_key_value_weight[1:],
        preferred_element_type=jnp.float32,
    ).astype(jnp.bfloat16)

    def cross_one(sample_queries, sample_keys, sample_values, lengths):
        allowed = (decoder_doc[:, None] == key_doc[None, :]) & live_keys(
            lengths, key_doc, key_place
        )[None, :]
        return attend(sample_queries, sample_keys, sample_values, allowed)

    mixture = jax.vmap(cross_one)(
        queries.reshape(micro_count, decoder_rows, cross_heads, HD),
        memory_heads[0].reshape(micro_count, row_count, cross_heads, HD),
        memory_heads[1].reshape(micro_count, row_count, cross_heads, HD),
        doc_lengths,
    )
    cross_terms = jnp.einsum(
        "brc,cd->brd",
        mixture.reshape(micro_count, decoder_rows, -1),
        w_cross_out,
        preferred_element_type=jnp.float32,
    )
    cross_sum = lax.psum(cross_terms, "section")
    closing_rows = norm_rows(docid_embed.astype(jnp.float32) + cross_sum, dec_gain[1]).astype(
        jnp.bfloat16
    )
    scores_vocab = jnp.einsum(
        "brd,dv->brv", closing_rows, docid_head_weight, preferred_element_type=jnp.float32
    )
    vocab_local = docid_head_weight.shape[1]
    vocab_start = section_index * vocab_local
    matches = docid_targets[..., None] == vocab_start + jnp.arange(vocab_local)
    exponent_total, picked = lax.psum(
        (
            jnp.sum(jnp.exp(scores_vocab), axis=-1),
            jnp.sum(jnp.where(matches, scores_vocab, 0.0), axis=-1),
        ),
        "section",
    )
    token_loss = jnp.log(exponent_total) - picked
    mean_loss = lax.psum(jnp.sum(token_loss), "rep") / (token_loss.size * lax.axis_size("rep"))
    return (scores_vocab.astype(jnp.bfloat16), token_loss, mean_loss)


def encoder_kernel(
    sent,
    x_ref,
    gain_ref,
    row_doc_ref,
    key_doc_ref,
    wqkv_ref,
    wout_ref,
    mem_ref,
    wqkv_v,
    wout_v,
    hid,
    work,
    part,
    qkv,
    mix,
    w_sem,
    o_sem,
    x_sem,
    gs,
    gr,
    rs,
    rr,
    zs,
    zr,
    bs,
    br,
    ms,
    mr,
):
    rows, width = hid.shape
    half = sent // 2
    columns = width // PARTS
    tiles = wqkv_v.shape[0]
    per = tiles // 3
    section = lax.axis_index("section")
    count = lax.axis_size("section")
    group = section // 2
    lane = section % 2
    partner = section + 1 - 2 * lane
    ahead = lax.rem(section + 2, count)
    behind = lax.rem(section + count - 2, count)
    own = pl.ds(pl.multiple_of(lane * half, 16), half)
    other = pl.ds(pl.multiple_of((1 - lane) * half, 16), half)

    def cols(c):
        return pl.ds(pl.multiple_of(c * columns, columns), columns)

    def weight_copy(j):
        return pltpu.make_async_copy(
            wqkv_ref.at[j // per, pl.ds((j % per) * WTILE, WTILE)], wqkv_v.at[j], w_sem.at[j]
        )

    def out_copy(c):
        return pltpu.make_async_copy(wout_ref.at[:, cols(c)], wout_v.at[c], o_sem.at[c])

    def remote(src, dst, send, recv, device):
        return pltpu.make_async_remote_copy(
            src_ref=src,
            dst_ref=dst,
            send_sem=send,
            recv_sem=recv,
            device_id={"section": device},
            device_id_type=MESH,
        )

    def gather(c, block):
        return remote(hid.at[block, cols(c)], hid.at[block, cols(c)], gs.at[c], gr.at[c], partner)

    def reduce(c):
        return remote(work.at[other, cols(c)], part.at[:, cols(c)], rs.at[c], rr.at[c], partner)

    def hand(c):
        return remote(hid.at[own, cols(c)], hid.at[own, cols(c)], zs.at[c], zr.at[c], ahead)

    def back(c):
        return remote(mem_ref.at[own, cols(c)], mem_ref.at[own, cols(c)], bs.at[c], br.at[c], behind)

    def spread(c, block):
        return remote(
            mem_ref.at[block, cols(c)], mem_ref.at[block, cols(c)], ms.at[c], mr.at[c], partner
        )

    def each(size, body):
        def step(i, carry):
            body(i)
            return carry

        lax.fori_loop(0, size, step, 0)

    entry = pltpu.make_async_copy(x_ref.at[pl.ds(0, sent)], hid.at[pl.ds(0, sent)], x_sem)

    @pl.when(group == 0)
    def _():
        entry.start()

    for j in range(tiles):
        weight_copy(j).start()
    for c in range(PARTS):
        out_copy(c).start()

    barrier = pltpu.get_barrier_semaphore()
    for device in (partner, ahead, behind):
        pl.semaphore_signal(barrier, inc=1, device_id={"section": device}, device_id_type=MESH)
    pl.semaphore_wait(barrier, 3)

    if sent < rows:
        hid[sent:, :] = jnp.zeros((rows - sent, width), hid.dtype)
    if sent < mem_ref.shape[0]:
        mem_ref[sent:, :] = jnp.zeros((mem_ref.shape[0] - sent, width), mem_ref.dtype)

    @pl.when(group == 0)
    def _():
        entry.wait()

    @pl.when(group > 0)
    def _():
        def arrive(c):
            hand(c).wait_recv()
            gather(c, own).start()

        each(PARTS, arrive)

        def complete(c):
            gather(c, other).wait_recv()
            gather(c, own).wait_send()

        each(PARTS, complete)

    def norm(r):
        block = pl.ds(pl.multiple_of(r * 16, 16), 16)
        values = hid[block, :].astype(jnp.float32)
        scale = lax.rsqrt(jnp.mean(values * values, axis=-1, keepdims=True) + 1e-06)
        work[block, :] = (values * scale * gain_ref[...]).astype(work.dtype)

    each(rows // 16, norm)

    def project(j):
        pltpu.make_async_copy(
            wqkv_ref.at[0, pl.ds(0, WTILE)], wqkv_v.at[j], w_sem.at[j]
        ).wait()
        qkv[j] = lax.dot_general(
            work[...], wqkv_v[j], (((1,), (1,)), ((), ())), preferred_element_type=jnp.float32
        ).astype(qkv.dtype)

    each(tiles, project)
    pairs = WTILE // (2 * HD)

    def attend_pair(p):
        tile = p // pairs
        span = pl.ds(pl.multiple_of((p % pairs) * 2 * HD, 2 * HD), 2 * HD)
        queries = qkv[tile, :, span]
        keys = qkv[per + tile, :, span]
        values = qkv[2 * per + tile, :, span]
        allowed = row_doc_ref[...] == key_doc_ref[...]
        first = lax.broadcasted_iota(jnp.int32, (rows, 2 * HD), 1) < HD
        mixed = []
        for side in range(2):
            keep = first if side == 0 else jnp.logical_not(first)
            chosen = jnp.where(keep, queries.astype(jnp.float32), 0.0).astype(jnp.bfloat16)
            scores = lax.dot_general(
                chosen, keys, (((1,), (1,)), ((), ())), preferred_element_type=jnp.float32
            )
            weights = jnp.where(allowed, jnp.exp(scores), 0.0)
            shares = (weights / jnp.sum(weights, axis=-1, keepdims=True)).astype(jnp.bfloat16)
            mixed.append(jnp.dot(shares, values, preferred_element_type=jnp.float32))
        mix[:, pl.ds(pl.multiple_of(p * 2 * HD, 2 * HD), 2 * HD)] = jnp.where(
            first, mixed[0], mixed[1]
        ).astype(mix.dtype)

    each(per * pairs, attend_pair)

    def output(c):
        out_copy(c).wait()
        work[:, cols(c)] = jnp.dot(
            mix[...], wout_v[c], preferred_element_type=jnp.float32
        ).astype(work.dtype)
        reduce(c).start()

    each(PARTS, output)

    def total(c):
        reduce(c).wait_recv()
        return (
            hid[own, cols(c)].astype(jnp.float32)
            + work[own, cols(c)].astype(jnp.float32)
            + part[:, cols(c)].astype(jnp.float32)
        ).astype(hid.dtype)

    @pl.when(group < GROUPS - 1)
    def _():
        def finish(c):
            hid[own, cols(c)] = total(c)
            hand(c).start()

        each(PARTS, finish)

        def relay(c):
            back(c).wait_recv()

            @pl.when(group > 0)
            def _():
                back(c).start()

            spread(c, own).start()

        each(PARTS, relay)

    @pl.when(group == GROUPS - 1)
    def _():
        def finish(c):
            mem_ref[own, cols(c)] = total(c)
            back(c).start()
            spread(c, own).start()

        each(PARTS, finish)

    def drain(c):
        spread(c, other).wait_recv()
        spread(c, own).wait_send()
        reduce(c).wait_send()

        @pl.when(group < GROUPS - 1)
        def _():
            hand(c).wait_send()

        @pl.when(group > 0)
        def _():
            back(c).wait_send()

    each(PARTS, drain)


def encode(rows, sent, number, x, gain, row_doc, key_doc, wqkv, wout):
    total_rows, width = x.shape
    inner = wout.shape[0]
    tiles = 3 * (inner // WTILE)
    dma = pltpu.SemaphoreType.DMA
    vmem = pl.BlockSpec(memory_space=pltpu.VMEM)
    anywhere = pl.BlockSpec(memory_space=pl.ANY)
    return pl.pallas_call(
        functools.partial(encoder_kernel, sent),
        out_shape=jax.ShapeDtypeStruct((total_rows, width), jnp.bfloat16),
        in_specs=[anywhere, vmem, vmem, vmem, anywhere, anywhere],
        out_specs=vmem,
        scratch_shapes=[
            pltpu.VMEM((tiles, WTILE, width), jnp.bfloat16),
            pltpu.VMEM((PARTS, inner, width // PARTS), jnp.bfloat16),
            pltpu.VMEM((rows, width), jnp.bfloat16),
            pltpu.VMEM((rows, width), jnp.bfloat16),
            pltpu.VMEM((sent // 2, width), jnp.bfloat16),
            pltpu.VMEM((tiles, rows, WTILE), jnp.bfloat16),
            pltpu.VMEM((rows, inner), jnp.bfloat16),
            dma((tiles,)),
            dma((PARTS,)),
            dma,
        ]
        + [dma((PARTS,))] * 10,
        compiler_params=pltpu.CompilerParams(
            collective_id=number, has_side_effects=True, vmem_limit_bytes=67043328
        ),
        name=f"encoder_{sent}",
    )(x, gain, row_doc[:rows, None], key_doc[None, :rows], wqkv, wout)


def stream_kernel(
    sent,
    x_ref,
    gain_ref,
    row_doc_ref,
    key_doc_ref,
    wqkv_ref,
    wout_ref,
    mem_ref,
    wqkv_v,
    wout_v,
    hid,
    work,
    part,
    acc,
    squares,
    mix,
    w_sem,
    o_sem,
    x_sem,
    gs,
    gr,
    rs,
    rr,
    zs,
    zr,
    bs,
    br,
    ms,
    mr,
):
    rows, width = hid.shape
    half = sent // 2
    chunks, tiles, tile_columns, columns = wqkv_v.shape
    per = tiles // 3
    section = lax.axis_index("section")
    count = lax.axis_size("section")
    group = section // 2
    lane = section % 2
    partner = section + 1 - 2 * lane
    ahead = lax.rem(section + 2, count)
    behind = lax.rem(section + count - 2, count)
    own = pl.ds(pl.multiple_of(lane * half, 16), half)
    other = pl.ds(pl.multiple_of((1 - lane) * half, 16), half)

    def cols(c):
        return pl.ds(pl.multiple_of(c * columns, columns), columns)

    def weight_copy(c):
        return pltpu.make_async_copy(wqkv_ref.at[:, :, cols(c)], wqkv_v.at[c], w_sem.at[c])

    def out_copy(c):
        return pltpu.make_async_copy(wout_ref.at[:, cols(c)], wout_v.at[c], o_sem.at[c])

    def remote(src, dst, send, recv, device):
        return pltpu.make_async_remote_copy(
            src_ref=src,
            dst_ref=dst,
            send_sem=send,
            recv_sem=recv,
            device_id={"section": device},
            device_id_type=MESH,
        )

    def gather(c, block):
        return remote(hid.at[block, cols(c)], hid.at[block, cols(c)], gs.at[c], gr.at[c], partner)

    def reduce(c):
        return remote(work.at[other, cols(c)], part.at[:, cols(c)], rs.at[c], rr.at[c], partner)

    def hand(c):
        return remote(hid.at[own, cols(c)], hid.at[own, cols(c)], zs.at[c], zr.at[c], ahead)

    def back(c):
        return remote(mem_ref.at[own, cols(c)], mem_ref.at[own, cols(c)], bs.at[c], br.at[c], behind)

    def spread(c, block):
        return remote(
            mem_ref.at[block, cols(c)], mem_ref.at[block, cols(c)], ms.at[c], mr.at[c], partner
        )

    def each(size, body):
        def step(i, carry):
            body(i)
            return carry

        lax.fori_loop(0, size, step, 0)

    entry = pltpu.make_async_copy(x_ref.at[pl.ds(0, sent)], hid.at[pl.ds(0, sent)], x_sem)

    @pl.when(group == 0)
    def _():
        entry.start()

    for c in range(chunks):
        weight_copy(c).start()
    for c in range(chunks):
        out_copy(c).start()

    barrier = pltpu.get_barrier_semaphore()
    for device in (partner, ahead, behind):
        pl.semaphore_signal(barrier, inc=1, device_id={"section": device}, device_id_type=MESH)
    pl.semaphore_wait(barrier, 3)

    if sent < rows:
        hid[sent:, :] = jnp.zeros((rows - sent, width), hid.dtype)
    if sent < mem_ref.shape[0]:
        mem_ref[sent:, :] = jnp.zeros((mem_ref.shape[0] - sent, width), mem_ref.dtype)
    acc[...] = jnp.zeros_like(acc)
    squares[...] = jnp.zeros_like(squares)

    def project(c, weight_dim):
        values = hid[:, cols(c)].astype(jnp.float32)
        squares[...] += jnp.sum(values * values, axis=-1, keepdims=True)
        scaled = (values * gain_ref[:, cols(c)]).astype(jnp.bfloat16)

        def some(t):
            for u in range(per):
                j = t * per + u
                acc[j] += lax.dot_general(
                    scaled,
                    wqkv_v[c, j],
                    (((1,), (weight_dim,)), ((), ())),
                    preferred_element_type=jnp.float32,
                )

        each(3, some)

    @pl.when(group == 0)
    def _():
        entry.wait()

        def first(c):
            weight_copy(c).wait()
            project(c, 1)

        each(chunks, first)

    @pl.when(group > 0)
    def _():
        side = tile_columns // 2

        def turn(c):
            weight_copy(c).wait()

            def block(j):
                whole = wqkv_v[c, j]
                for a in range(2):
                    for b in range(2):
                        piece = whole[a * side : (a + 1) * side, b * side : (b + 1) * side]
                        wqkv_v[c, j, b * side : (b + 1) * side, a * side : (a + 1) * side] = piece.T

            each(tiles, block)

        each(chunks, turn)

        def step(i):
            @pl.when(i < chunks)
            def _():
                hand(i).wait_recv()
                gather(i, own).start()

            @pl.when(i >= AHEAD)
            def _():
                gather(i - AHEAD, other).wait_recv()
                project(i - AHEAD, 0)

        each(chunks + AHEAD, step)

        def complete(c):
            gather(c, own).wait_send()

        each(chunks, complete)

    scale = lax.rsqrt(squares[...] * (1.0 / width) + 1e-06)
    pairs = tile_columns // (2 * HD)
    allowed = row_doc_ref[...] == key_doc_ref[...]
    allowed = jnp.concatenate([allowed, allowed], 0)
    first = lax.broadcasted_iota(jnp.int32, (rows, 2 * HD), 1) < HD

    def attend_tile(tile):
        for p in range(pairs):
            span = slice(p * 2 * HD, (p + 1) * 2 * HD)
            queries = acc[tile, :, span] * scale
            keys = (acc[per + tile, :, span] * scale).astype(jnp.bfloat16)
            values = (acc[2 * per + tile, :, span] * scale).astype(jnp.bfloat16)
            both = jnp.concatenate(
                [jnp.where(first, queries, 0.0), jnp.where(first, 0.0, queries)], 0
            ).astype(jnp.bfloat16)
            scores = lax.dot_general(
                both, keys, (((1,), (1,)), ((), ())), preferred_element_type=jnp.float32
            )
            weights = jnp.where(allowed, jnp.exp(scores), 0.0)
            shares = weights * (1.0 / jnp.sum(weights, axis=-1, keepdims=True))
            mixed = jnp.dot(shares.astype(jnp.bfloat16), values, preferred_element_type=jnp.float32)
            place = pl.multiple_of(tile * tile_columns + p * 2 * HD, 2 * HD)
            mix[:, pl.ds(place, 2 * HD)] = jnp.where(first, mixed[:rows], mixed[rows:]).astype(
                mix.dtype
            )

    each(per, attend_tile)

    def output(c):
        out_copy(c).wait()
        work[:, cols(c)] = jnp.dot(
            mix[...], wout_v[c], preferred_element_type=jnp.float32
        ).astype(work.dtype)
        reduce(c).start()

    each(chunks, output)

    def total(c):
        reduce(c).wait_recv()
        return (
            hid[own, cols(c)].astype(jnp.float32)
            + work[own, cols(c)].astype(jnp.float32)
            + part[:, cols(c)].astype(jnp.float32)
        ).astype(hid.dtype)

    @pl.when(group < GROUPS - 1)
    def _():
        def finish(c):
            hid[own, cols(c)] = total(c)
            hand(c).start()

        each(chunks, finish)

        def relay(c):
            back(c).wait_recv()

            @pl.when(group > 0)
            def _():
                back(c).start()

            spread(c, own).start()

        each(chunks, relay)

    @pl.when(group == GROUPS - 1)
    def _():
        def finish(c):
            mem_ref[own, cols(c)] = total(c)
            back(c).start()
            spread(c, own).start()

        each(chunks, finish)

    def drain(c):
        spread(c, other).wait_recv()
        spread(c, own).wait_send()
        reduce(c).wait_send()

        @pl.when(group < GROUPS - 1)
        def _():
            hand(c).wait_send()

        @pl.when(group > 0)
        def _():
            back(c).wait_send()

    each(chunks, drain)


def stream(rows, sent, number, x, gain, row_doc, key_doc, wqkv, wout):
    total_rows, width = x.shape
    inner = wout.shape[0]
    tiles = 3 * (inner // WTILE)
    dma = pltpu.SemaphoreType.DMA
    vmem = pl.BlockSpec(memory_space=pltpu.VMEM)
    anywhere = pl.BlockSpec(memory_space=pl.ANY)
    return pl.pallas_call(
        functools.partial(stream_kernel, sent),
        out_shape=jax.ShapeDtypeStruct((total_rows, width), jnp.bfloat16),
        in_specs=[anywhere, vmem, vmem, vmem, anywhere, anywhere],
        out_specs=vmem,
        scratch_shapes=[
            pltpu.VMEM((CHUNKS, tiles, WTILE, width // CHUNKS), jnp.bfloat16),
            pltpu.VMEM((CHUNKS, inner, width // CHUNKS), jnp.bfloat16),
            pltpu.VMEM((rows, width), jnp.bfloat16),
            pltpu.VMEM((rows, width), jnp.bfloat16),
            pltpu.VMEM((sent // 2, width), jnp.bfloat16),
            pltpu.VMEM((tiles, rows, WTILE), jnp.float32),
            pltpu.VMEM((rows, 1), jnp.float32),
            pltpu.VMEM((rows, inner), jnp.bfloat16),
            dma((CHUNKS,)),
            dma((CHUNKS,)),
            dma,
        ]
        + [dma((CHUNKS,))] * 10,
        compiler_params=pltpu.CompilerParams(
            collective_id=number, has_side_effects=True, vmem_limit_bytes=67043328
        ),
        name=f"stream_{sent}",
    )(x, gain, row_doc[:rows, None], key_doc[None, :rows], wqkv.reshape(tiles, WTILE, width), wout)


def butterfly(value, axis, combine):
    for bit in range(lax.axis_size(axis).bit_length() - 1):
        value = combine(value, from_partner(value, axis, bit))
    return value


def greet(me, count):
    barrier = pltpu.get_barrier_semaphore()
    for k in range(1, count):
        pl.semaphore_signal(
            barrier, inc=1, device_id={"section": lax.rem(me + k, count)}, device_id_type=MESH
        )
    pl.semaphore_wait(barrier, count - 1)


def to_peer(src, dst, send, recv, peer):
    return pltpu.make_async_remote_copy(
        src_ref=src,
        dst_ref=dst,
        send_sem=send,
        recv_sem=recv,
        device_id={"section": peer},
        device_id_type=MESH,
    )


def closing_kernel(terms, residual, gain, out, landed, s1, r1, s2, r2):
    count = terms.shape[0]
    me = lax.axis_index("section")
    greet(me, count)

    def scatter(k, slot):
        peer = lax.rem(me + k, count)
        return to_peer(terms.at[peer], landed.at[slot], s1.at[k], r1.at[k], peer)

    def gather(k, slot):
        return to_peer(out.at[slot], out.at[slot], s2.at[k], r2.at[k], lax.rem(me + k, count))

    for k in range(1, count):
        scatter(k, me).start()
    total = residual[...] + terms[me].astype(jnp.float32)
    for k in range(1, count):
        slot = lax.rem(me + count - k, count)
        scatter(k, slot).wait_recv()
        total = total + landed[slot].astype(jnp.float32)
    scale = lax.rsqrt(jnp.mean(total * total, axis=-1, keepdims=True) + 1e-06)
    out[me] = (total * scale * gain[...]).astype(out.dtype)
    for k in range(1, count):
        gather(k, me).start()
    for k in range(1, count):
        gather(k, lax.rem(me + count - k, count)).wait_recv()
    for k in range(1, count):
        scatter(k, me).wait_send()
        gather(k, me).wait_send()


def closing_rows_of(terms, residual, gain):
    count = terms.shape[0]
    dma = pltpu.SemaphoreType.DMA
    vmem = pl.BlockSpec(memory_space=pltpu.VMEM)
    return pl.pallas_call(
        closing_kernel,
        out_shape=jax.ShapeDtypeStruct(terms.shape, jnp.bfloat16),
        in_specs=[vmem] * 3,
        out_specs=vmem,
        scratch_shapes=[pltpu.VMEM(terms.shape, jnp.bfloat16)] + [dma((count,))] * 4,
        compiler_params=pltpu.CompilerParams(collective_id=8, has_side_effects=True),
        name="closing",
    )(terms, residual, gain)


def sums_kernel(value, out, landed, send, recv):
    count = landed.shape[0]
    me = lax.axis_index("section")
    greet(me, count)

    def share(k, slot):
        return to_peer(value, landed.at[slot], send.at[k], recv.at[k], lax.rem(me + k, count))

    for k in range(1, count):
        share(k, me).start()
    landed[me] = value[...]
    for k in range(1, count):
        share(k, lax.rem(me + count - k, count)).wait_recv()
    total = landed[0]
    for k in range(1, count):
        total = total + landed[k]
    out[...] = total
    for k in range(1, count):
        share(k, me).wait_send()


def section_sum(value, count):
    dma = pltpu.SemaphoreType.DMA
    vmem = pl.BlockSpec(memory_space=pltpu.VMEM)
    return pl.pallas_call(
        sums_kernel,
        out_shape=jax.ShapeDtypeStruct(value.shape, value.dtype),
        in_specs=[vmem],
        out_specs=vmem,
        scratch_shapes=[pltpu.VMEM((count,) + value.shape, value.dtype)] + [dma((count,))] * 2,
        compiler_params=pltpu.CompilerParams(collective_id=9, has_side_effects=True),
        name="section_sum",
    )(value)


def fast_shards(
    document_token_embedding,
    doc_lengths,
    docid_embed,
    docid_targets,
    enc_gain,
    dec_gain,
    w_enc_qkv,
    w_enc_out,
    cross_query_key_value_weight,
    w_cross_out,
    docid_head_weight,
):
    section_index = lax.axis_index("section")
    group_index = section_index // 2
    micro_count, row_count, width = document_token_embedding.shape
    doc_count = doc_lengths.shape[1]
    doc_span = row_count // doc_count
    all_rows = micro_count * row_count
    positions = jnp.arange(all_rows)
    lengths = doc_lengths.reshape(-1)
    live = (jnp.arange(doc_span)[None, :] < lengths[:, None]).reshape(-1)
    ends = jnp.cumsum(lengths)
    live_count = ends[-1]
    starts = jnp.concatenate([jnp.zeros((1,), ends.dtype), ends[:-1]])
    inside = (positions[:, None] >= starts[None, :]) & (positions[:, None] < ends[None, :])
    docs = jnp.arange(lengths.shape[0])
    row_doc = jnp.sum(jnp.where(inside, docs[None, :], 0), axis=1).astype(jnp.int32)
    key_doc = jnp.where(positions < live_count, row_doc, -1).astype(jnp.int32)
    source = jnp.sum(
        jnp.where(inside, docs[None, :] * doc_span + positions[:, None] - starts[None, :], 0), axis=1
    )
    source = jnp.where(positions < live_count, source, -1)
    pick = (source[:, None] == positions[None, :]).astype(jnp.bfloat16)
    packed = jnp.dot(
        pick,
        document_token_embedding.reshape(all_rows, width),
        preferred_element_type=jnp.float32,
    ).astype(jnp.bfloat16)
    largest = butterfly(live_count.astype(jnp.float32)[None], "rep", jnp.maximum)[0]
    gain = lax.dynamic_slice_in_dim(enc_gain, group_index, 1, 0)
    unit = all_rows // 2
    sizes = [(unit, unit * 3 // 4), (unit, unit), (all_rows, all_rows)]
    choice = jnp.sum(jnp.stack([(largest > sent).astype(jnp.int32) for _, sent in sizes[:-1]]))
    branches = [
        functools.partial(encode if rows > unit else stream, rows, sent, number)
        for number, (rows, sent) in enumerate(sizes)
    ]
    hidden = lax.switch(
        choice, branches, packed, gain, row_doc, key_doc, w_enc_qkv, w_enc_out
    )
    memory = norm_rows(hidden, enc_gain[GROUPS]).astype(jnp.bfloat16)

    decoder_rows = docid_embed.shape[1]
    every = micro_count * decoder_rows
    docid_span = decoder_rows // doc_count
    decoder_doc = jnp.arange(every) // docid_span
    cross_heads = cross_query_key_value_weight.shape[1] // HD
    flat_docid = docid_embed.reshape(every, width)
    dec_normed = norm_rows(flat_docid, dec_gain[0]).astype(jnp.bfloat16)

    def project(values, weight):
        return (
            jnp.einsum("rd,cd->rc", values, weight, preferred_element_type=jnp.float32)
            .astype(jnp.bfloat16)
            .reshape(-1, cross_heads, HD)
        )

    queries = project(dec_normed, cross_query_key_value_weight[0])
    keys = project(memory, cross_query_key_value_weight[1])
    values = project(memory, cross_query_key_value_weight[2])
    allowed = decoder_doc[:, None] == key_doc[None, :]
    mixture = attend(queries, keys, values, allowed).reshape(every, -1)
    cross_terms = jnp.dot(mixture, w_cross_out, preferred_element_type=jnp.float32)
    section_count = lax.axis_size("section")
    share = every // section_count
    residual = lax.dynamic_slice_in_dim(flat_docid, section_index * share, share, 0)
    closing = closing_rows_of(
        cross_terms.astype(jnp.bfloat16).reshape(section_count, share, width),
        residual.astype(jnp.float32),
        dec_gain[1:2],
    ).reshape(every, width)
    scores_vocab = jnp.dot(closing, docid_head_weight, preferred_element_type=jnp.float32)
    vocab_local = docid_head_weight.shape[1]
    targets = docid_targets.reshape(-1)
    matches = targets[:, None] == section_index * vocab_local + jnp.arange(vocab_local)
    sums = jnp.stack(
        [
            jnp.sum(jnp.exp(scores_vocab), axis=-1),
            jnp.sum(jnp.where(matches, scores_vocab, 0.0), axis=-1),
        ]
    )
    padding = ((0, -sums.shape[0] % 8), (0, -sums.shape[1] % 128))
    sums = section_sum(jnp.pad(sums, padding), section_count)[:2, :every]
    token_loss = jnp.log(sums[0]) - sums[1]
    loss_sum = butterfly(jnp.sum(token_loss)[None], "rep", jnp.add)[0]
    mean_loss = loss_sum / (token_loss.size * lax.axis_size("rep"))
    logits = scores_vocab.astype(jnp.bfloat16).reshape(micro_count, decoder_rows, vocab_local)
    return (logits, token_loss.reshape(docid_targets.shape), mean_loss)


def solution(mesh):
    in_specs = (
        P("rep", None, None),
        P("rep", None),
        P("rep", None, None),
        P("rep", None),
        P(),
        P(),
        P(None, "section", None),
        P("section", None),
        P(None, "section", None),
        P("section", None),
        P(None, "section"),
    )
    out_specs = (P("rep", None, "section"), P("rep", None), P())
    local = shards if mesh.shape["section"] != 2 * GROUPS else fast_shards
    return jax.shard_map(local, mesh=mesh, in_specs=in_specs, out_specs=out_specs, check_vma=False)
```

profile of v0, /device:TPU:0, one launch (start us, length us, event | category | flops | bytes accessed | tf_op | source)
XLA Modules:
  0.0 219.0 jit_solution(16397602772990046681)
XLA Ops:
  0.6 0.0 copy-start.5
  0.6 0.0 copy-start.1
  0.7 0.8 reshape.166
  1.5 0.2 reduce-window.4
  1.7 0.6 slice.49
  2.9 1.4 collective-permute-start
  4.3 1.6 fusion.38
  5.9 0.1 pad_add_fusion
  6.0 0.1 select_reduce_fusion.1
  6.1 0.6 fusion.33
  6.7 3.7 %convolution_convert_fusion = bf16[256,4096]{1,0:T(8,128)(2,1)} fusion(bf16[256,4096]{1,0:T(8,128)(2,1)} %bitcast.70, s32[256]{0:T(256)S(1)} %get-tuple-element.83), kind=kOutput, calls=%fused_computation.7 | convolution fusion | flops 537985024 | bytes 4195328 | tf_op jit(solution)/shard_map/dot_general | solution.py:921
  10.4 0.0 copy-start.9
  10.4 0.7 broadcast_compare_fusion
  11.1 0.0 copy-done.5
  11.1 0.6 fusion.39
  11.7 0.0 copy-done.1
  11.7 0.2 fusion.20
  11.9 0.2 fusion.22
  12.1 3.6 %fusion.17 = bf16[64,512]{1,0:T(8,128)(2,1)S(1)} fusion(bf16[64,4096]{1,0:T(8,128)(2,1)S(1)} %bitcast.72, bf16[3,512,4096]{2,1,0:T(8,128)(2,1)} %param.22), kind=kOutput, calls=%fused_computation.27 | convolution fusion | flops 268468224 | bytes 4784128 | tf_op jit(solution)/shard_map/rd,cd->rc/dot_general | solution.py:950
  15.7 0.8 reshape.169
  16.5 0.6 iota_add_fusion
  17.1 0.0 copy-done.9
  17.1 0.6 eq.51
  17.7 0.7 dynamic-slice_convert_fusion.residual
  18.4 0.0 collective-permute-done
  19.0 3.8 %collective-permute-start.1 = (f32[1]{0:T(128)}, f32[1]{0:T(128)}, u32[]{:S(2)}, u32[]{:S(2)}) collective-permute-start(f32[1]{0:T(128)} %max.6), channel_id=1, source_target_pairs={{0,2},{2,0},{1,3},{3,1},{4,6},{6,4},{5,7},{7,5},{8,10},{10,8},{9,1... | collective-permute-start | bytes 20 | tf_op jit(solution)/shard_map/ppermute | solution.py:26
  22.8 0.2 collective-permute-done.1
  23.7 133.7 %conditional.2 = (bf16[256,4096]{1,0:T(8,128)(2,1)}, f32[256,1]{0,1:T(1,128)S(1)}) conditional(s32[]{:T(128)} %bitcast.13, (s32[256]{0:T(256)S(1)}, s32[256]{0:T(256)S(1)}, bf16[3,1536,4096]{2,1,0:T(8,128)(2,1)}, bf16[256,4096]{1,0:T(8,128)(2,1)}, f32[1,4096]{1,0:T(1,128)}, /*index=5*/bf16[1536,4096]{1,0:T(8,128)(2,1)}) %tuple.27, ...), branch_computations={%region_3.5_spmd, %region_5.7_spmd, %region_7.9_spmd} | conditional | flops 3145472 | bytes 2104364
  23.7 0.5 slice_bitcast_fusion
  24.2 0.7 copy.25.row_doc_ref
  24.9 130.2 %stream_96.1 = bf16[256,4096]{1,0:T(8,128)(2,1)} custom-call(bf16[256,4096]{1,0:T(8,128)(2,1)} %get-tuple-element.42.x_ref, f32[1,4096]{1,0:T(1,128)} %get-tuple-element.43.gain_ref, s32[128,1]{1,0:T(8,128)} %copy.25.row_doc_ref, s32[1,128]{1,0:T(1,128)} %get-tuple-element.73.key_doc_ref, bf16[9,512,4096]{2,1,0:T(8,128)(2,1)} %bitcast.67, ...), custom_call_target="tpu_custom_call" | custom-call | tf_op jit(solution)/shard_map/cond/branch_0_fun/stream_96/pallas_call | solution.py:755
  155.1 2.1 multiply_reduce_fusion
  157.4 0.0 copy-start
  157.4 0.0 copy-start.7
  157.4 4.3 %fusion.14 = bf16[256,512]{1,0:T(8,128)(2,1)S(1)} fusion(bf16[3,512,4096]{2,1,0:T(8,128)(2,1)} %param.22, bf16[256,4096]{1,0:T(8,128)(2,1)} %get-tuple-element.65, f32[4096]{0:T(1024)} %bitcast.79, f32[256]{0:T(256)S(1)} %bitcast.86), kind=kOutput, calls=%fused_computation.25 | convolution fusion | flops 1078067200 | bytes 6571008 | tf_op jit(solution)/shard_map/rd,cd->rc/dot_general | solution.py:950
  161.7 0.0 copy-done
  161.7 0.0 copy-done.7
  161.7 0.0 copy-start.2
  161.7 0.0 copy-start.3
  161.7 3.5 %fusion.11 = bf16[256,512]{1,0:T(8,128)(2,1)S(1)} fusion(bf16[3,512,4096]{2,1,0:T(8,128)(2,1)} %param.22, bf16[256,4096]{1,0:T(8,128)(2,1)S(1)} %copy-done, f32[4096]{0:T(1024)S(1)} %bitcast.80, f32[256]{0:T(256)S(1)} %bitcast.87), kind=kOutput, calls=%fused_computation.24 | convolution fusion | flops 1078067200 | bytes 6571008 | tf_op jit(solution)/shard_map/rd,cd->rc/dot_general | solution.py:950
  165.3 0.1 copy.29
  165.4 0.1 copy.28
  165.5 0.0 copy-done.2
  165.6 0.0 copy-done.3
  165.6 0.2 fusion.10
  165.8 0.0 copy-start.4
  165.8 0.0 copy-start.8
  165.8 0.3 convolution_convert_fusion.2
  166.1 3.9 %fusion.terms = bf16[8,8,4096]{2,1,0:T(8,128)(2,1)} fusion(bf16[64,512]{0,1:T(8,128)(2,1)S(1)} %bitcast.75, bf16[512,4096]{1,0:T(8,128)(2,1)} %param.23), kind=kOutput, calls=%fused_computation.9 | convolution fusion | flops 268697600 | bytes 4784128 | tf_op jit(solution)/shard_map/dot_general | solution.py:960
  170.0 19.0 %closing.1 = bf16[8,8,4096]{2,1,0:T(8,128)(2,1)} custom-call(bf16[8,8,4096]{2,1,0:T(8,128)(2,1)} %fusion.terms, f32[8,4096]{1,0:T(8,128)} %dynamic-slice_convert_fusion.residual, f32[1,4096]{1,0:T(1,128)} %get-tuple-element.80.gain), custom_call_target="tpu_custom_call" | custom-call | tf_op jit(solution)/shard_map/closing/pallas_call | solution.py:841
  189.0 0.0 copy-done.4
  189.0 0.0 copy-done.8
  189.0 9.8 %exponential_reduce_fusion = (f32[64]{0:T(128)S(1)}, f32[64]{0:T(128)S(1)}, bf16[64,2048]{1,0:T(8,128)(2,1)}) fusion(s32[2048]{0:T(1024)S(1)} %copy-done.4, s32[64]{0:T(128)S(1)} %copy-done.8, bf16[4096,2048]{1,0:T(8,128)(2,1)} %param.24, bf16[8,8,4096]{2,1,0:T(8,128)(2,1)} %closing.1), kind=kOutput, calls=%fused_computation.34 | convolution fusion | flops 1074397184 | bytes 17572608 | tf_op jit(solution)/shard_map/dot_general | solution.py:969
  198.9 0.6 select_maximum_fusion.value
  199.5 8.9 %section_sum.1 = f32[8,128]{1,0:T(8,128)} custom-call(f32[8,128]{1,0:T(8,128)} %select_maximum_fusion.value), custom_call_target="tpu_custom_call" | custom-call | tf_op jit(solution)/shard_map/section_sum/pallas_call | solution.py:876
  208.4 0.5 broadcast.118
  208.9 2.0 fusion.37
  210.9 0.0 collective-permute-start.2
  210.9 0.6 sub.28
  211.6 0.6 collective-permute-done.2
  213.6 2.9 %collective-permute-start.3 = (f32[1]{0:T(128)}, f32[1]{0:T(128)}, u32[]{:S(2)}, u32[]{:S(2)}) collective-permute-start(f32[1]{0:T(128)} %add.70), channel_id=1, source_target_pairs={{0,2},{2,0},{1,3},{3,1},{4,6},{6,4},{5,7},{7,5},{8,10},{10,8},{9,1... | collective-permute-start | bytes 20 | tf_op jit(solution)/shard_map/ppermute | solution.py:26
  216.4 0.7 collective-permute-done.3
  (5 shorter events, 0.0 us)
Async XLA Ops:
  0.6 10.5 %copy-start.5 = (f32[2,4096]{1,0:T(2,128)S(1)}, f32[2,4096]{1,0:T(2,128)}, u32[]{:S(2)}) copy-start(f32[2,4096]{1,0:T(2,128)} %param.19) | copy-start | bytes 98308
  0.6 11.1 %copy-start.1 = (bf16[2,32,4096]{2,1,0:T(8,128)(2,1)S(1)}, bf16[2,32,4096]{2,1,0:T(8,128)(2,1)}, u32[]{:S(2)}) copy-start(bf16[2,32,4096]{2,1,0:T(8,128)(2,1)} %param.16) | copy-start | bytes 1572868
  2.9 15.5 %collective-permute-start = (f32[1]{0:T(128)}, f32[1]{0:T(128)}, u32[]{:S(2)}, u32[]{:S(2)}) collective-permute-start(f32[1]{0:T(128)} %bitcast.12), channel_id=1, source_target_pairs={{0,1},{1,0},{2,3},{3,2},{4,5},{5,4},{6,7},{7,6},{8,9},{9,8},{10,11... | collective-permute-start | bytes 20 | tf_op jit(solution)/shard_map/ppermute | solution.py:26
  10.4 6.7 %copy-start.9 = (s32[2,32]{1,0:T(2,128)S(1)}, s32[2,32]{1,0:T(2,128)}, u32[]{:S(2)}) copy-start(s32[2,32]{1,0:T(2,128)} %param.17) | copy-start | bytes 772
  19.0 4.0 %collective-permute-start.1 = (f32[1]{0:T(128)}, f32[1]{0:T(128)}, u32[]{:S(2)}, u32[]{:S(2)}) collective-permute-start(f32[1]{0:T(128)} %max.6), channel_id=1, source_target_pairs={{0,2},{2,0},{1,3},{3,1},{4,6},{6,4},{5,7},{7,5},{8,10},{10,8},{9,1... | collective-permute-start | bytes 20 | tf_op jit(solution)/shard_map/ppermute | solution.py:26
  157.4 4.3 %copy-start = (bf16[256,4096]{1,0:T(8,128)(2,1)S(1)}, bf16[256,4096]{1,0:T(8,128)(2,1)}, u32[]{:S(2)}) copy-start(bf16[256,4096]{1,0:T(8,128)(2,1)} %get-tuple-element.65) | copy-start | bytes 6291460
  157.4 4.3 %copy-start.7 = (f32[1,4096]{1,0:T(1,128)S(1)}, f32[1,4096]{1,0:T(1,128)}, u32[]{:S(2)}) copy-start(f32[1,4096]{1,0:T(1,128)} %get-tuple-element.78) | copy-start | bytes 49156
  161.7 3.8 %copy-start.2 = (bf16[64,8,64]{2,1,0:T(8,128)(2,1)S(1)}, bf16[64,8,64]{2,1,0:T(8,128)(2,1)}, u32[]{:S(2)}) copy-start(bf16[64,8,64]{2,1,0:T(8,128)(2,1)} %reshape.169) | copy-start | bytes 196612
  161.7 3.8 %copy-start.3 = (pred[64,256]{1,0:T(8,128)(4,1)S(1)}, pred[64,256]{1,0:T(8,128)(4,1)}, u32[]{:S(2)}) copy-start(pred[64,256]{1,0:T(8,128)(4,1)} %broadcast_compare_fusion) | copy-start | bytes 49156
  165.8 23.2 %copy-start.4 = (s32[2048]{0:T(1024)S(1)}, s32[2048]{0:T(1024)}, u32[]{:S(2)}) copy-start(s32[2048]{0:T(1024)} %iota_add_fusion) | copy-start | bytes 24580
  165.8 23.2 %copy-start.8 = (s32[64]{0:T(128)S(1)}, s32[64]{0:T(128)}, u32[]{:S(2)}) copy-start(s32[64]{0:T(128)} %eq.51) | copy-start | bytes 772
  210.9 1.3 collective-permute-start.2
  213.6 3.6 %collective-permute-start.3 = (f32[1]{0:T(128)}, f32[1]{0:T(128)}, u32[]{:S(2)}, u32[]{:S(2)}) collective-permute-start(f32[1]{0:T(128)} %add.70), channel_id=1, source_target_pairs={{0,2},{2,0},{1,3},{3,1},{4,6},{6,4},{5,7},{7,5},{8,10},{10,8},{9,1... | collective-permute-start | bytes 20 | tf_op jit(solution)/shard_map/ppermute | solution.py:26
where the time goes:
time: 219 us
  Pallas kernels  158 us (72%)
  matrix products  29.3 us (13%)
  starting transfers between devices  8.07 us (4%)
  other arithmetic  8.03 us (4%)
  local copies, waits for them, and re-layouts  7.74 us (4%)
  between operations  5.9 us (3%)
    pallas_call x1, Pallas kernels, stream(): pl.pallas_call(functools.partial(stream_kernel, sent), out_shape=jax.Shap...  130 us
    pallas_call x1, Pallas kernels, closing_rows_of(): pl.pallas_call(closing_kernel, out_shape=jax.ShapeDtypeStruct(terms.shape...  19 us
    dot_general x3, matrix products, project(): jnp.einsum('rd,cd->rc', values, weight, preferred_element_type=jnp.float32)  11.4 us
    dot_general x1, matrix products, fast_shards(): jnp.dot(closing, docid_head_weight, preferred_element_type=jnp.float32)  9.83 us
    pallas_call x1, Pallas kernels, section_sum(): pl.pallas_call(sums_kernel, out_shape=jax.ShapeDtypeStruct(value.shape, v...  8.93 us
    ppermute x4, starting transfers between devices, from_partner(): return lax.ppermute(block, axis, route)  8.07 us
  transfers between devices with their start and end apart: 4, of which 3 were waited for; matrix products, arithmetic and copies ran while one was open for 7% of the time, Pallas kernels for 0%

commit v1 on v0

--- a/solution.py
+++ b/solution.py
@@ -484,21 +484,39 @@
 
 def stream_kernel(
     sent,
+    lengths_ref,
     x_ref,
-    gain_ref,
-    row_doc_ref,
-    key_doc_ref,
+    enc_gain_ref,
+    dec_gain_ref,
+    docid_ref,
+    target_ref,
     wqkv_ref,
     wout_ref,
-    mem_ref,
+    wcross_ref,
+    wclose_ref,
+    whead_ref,
+    logits_ref,
+    loss_ref,
+    mean_ref,
     wqkv_v,
     wout_v,
+    entered,
     hid,
     work,
     part,
     acc,
     squares,
     mix,
+    memory,
+    cross_acc,
+    query_acc,
+    terms,
+    landed,
+    closing,
+    scores,
+    stats,
+    stats_landed,
+    loss_landed,
     w_sem,
     o_sem,
     x_sem,
@@ -512,13 +530,32 @@
     br,
     ms,
     mr,
+    k_sem,
+    q_sem,
+    c_sem,
+    h_sem,
+    ts,
+    tr,
+    fs,
+    fr,
+    ss,
+    sr,
+    ls,
+    lr,
 ):
     rows, width = hid.shape
     half = sent // 2
     chunks, tiles, tile_columns, columns = wqkv_v.shape
     per = tiles // 3
+    doc_total = lengths_ref.shape[0]
+    doc_span = x_ref.shape[0] // doc_total
+    share_count, share, _ = docid_ref.shape
+    every = share_count * share
+    blocks = whead_ref.shape[1] // tile_columns
     section = lax.axis_index("section")
     count = lax.axis_size("section")
+    rep = lax.axis_index("rep")
+    rep_count = lax.axis_size("rep")
     group = section // 2
     lane = section % 2
     partner = section + 1 - 2 * lane
@@ -535,6 +572,29 @@
 
     def out_copy(c):
         return pltpu.make_async_copy(wout_ref.at[:, cols(c)], wout_v.at[c], o_sem.at[c])
+
+    def entry_copy(c):
+        return pltpu.make_async_copy(x_ref.at[:, cols(c)], entered.at[:, cols(c)], x_sem.at[c])
+
+    def key_copy(c):
+        return pltpu.make_async_copy(
+            wcross_ref.at[pl.ds(1, 2), :, cols(c)], wqkv_v.at[c, pl.ds(0, 2)], k_sem.at[c]
+        )
+
+    def query_copy(c):
+        return pltpu.make_async_copy(wcross_ref.at[0, :, cols(c)], wqkv_v.at[c, 2], q_sem.at[c])
+
+    def close_copy(c):
+        return pltpu.make_async_copy(wclose_ref.at[:, cols(c)], wqkv_v.at[c, 3], c_sem.at[c])
+
+    def head_copy(i):
+        c = i // blocks
+        b = i % blocks
+        return pltpu.make_async_copy(
+            whead_ref.at[cols(c), pl.ds(pl.multiple_of(b * tile_columns, 128), tile_columns)],
+            wqkv_v.at[c, 4 + b],
+            h_sem.at[i],
+        )
 
     def remote(src, dst, send, recv, device):
         return pltpu.make_async_remote_copy(
@@ -556,11 +616,36 @@
         return remote(hid.at[own, cols(c)], hid.at[own, cols(c)], zs.at[c], zr.at[c], ahead)
 
     def back(c):
-        return remote(mem_ref.at[own, cols(c)], mem_ref.at[own, cols(c)], bs.at[c], br.at[c], behind)
+        return remote(memory.at[own, cols(c)], memory.at[own, cols(c)], bs.at[c], br.at[c], behind)
 
     def spread(c, block):
         return remote(
-            mem_ref.at[block, cols(c)], mem_ref.at[block, cols(c)], ms.at[c], mr.at[c], partner
+            memory.at[block, cols(c)], memory.at[block, cols(c)], ms.at[c], mr.at[c], partner
+        )
+
+    def peer(k):
+        return lax.rem(section + k, count)
+
+    def source_of(k):
+        return lax.rem(section + count - k, count)
+
+    def scatter(k, slot):
+        return remote(terms.at[peer(k)], landed.at[slot], ts.at[k], tr.at[k], peer(k))
+
+    def collect(k, slot):
+        return remote(closing.at[slot], closing.at[slot], fs.at[k], fr.at[k], peer(k))
+
+    def share_stats(k, slot):
+        return remote(stats, stats_landed.at[slot], ss.at[k], sr.at[k], peer(k))
+
+    def share_loss(k, slot):
+        return pltpu.make_async_remote_copy(
+            src_ref=loss_ref,
+            dst_ref=loss_landed.at[slot],
+            send_sem=ls.at[k],
+            recv_sem=lr.at[k],
+            device_id={"rep": lax.rem(rep + k, rep_count)},
+            device_id_type=MESH,
         )
 
     def each(size, body):
@@ -570,11 +655,10 @@
 
         lax.fori_loop(0, size, step, 0)
 
-    entry = pltpu.make_async_copy(x_ref.at[pl.ds(0, sent)], hid.at[pl.ds(0, sent)], x_sem)
-
     @pl.when(group == 0)
     def _():
-        entry.start()
+        for c in range(chunks):
+            entry_copy(c).start()
 
     for c in range(chunks):
         weight_copy(c).start()
@@ -582,21 +666,44 @@
         out_copy(c).start()
 
     barrier = pltpu.get_barrier_semaphore()
-    for device in (partner, ahead, behind):
-        pl.semaphore_signal(barrier, inc=1, device_id={"section": device}, device_id_type=MESH)
-    pl.semaphore_wait(barrier, 3)
+    for k in range(1, count):
+        pl.semaphore_signal(barrier, inc=1, device_id={"section": peer(k)}, device_id_type=MESH)
+    for k in range(1, rep_count):
+        pl.semaphore_signal(
+            barrier, inc=1, device_id={"rep": lax.rem(rep + k, rep_count)}, device_id_type=MESH
+        )
+    pl.semaphore_wait(barrier, count + rep_count - 2)
 
     if sent < rows:
         hid[sent:, :] = jnp.zeros((rows - sent, width), hid.dtype)
-    if sent < mem_ref.shape[0]:
-        mem_ref[sent:, :] = jnp.zeros((mem_ref.shape[0] - sent, width), mem_ref.dtype)
+        memory[sent:, :] = jnp.zeros((rows - sent, width), memory.dtype)
     acc[...] = jnp.zeros_like(acc)
+    cross_acc[...] = jnp.zeros_like(cross_acc)
+    query_acc[...] = jnp.zeros_like(query_acc)
+    scores[...] = jnp.zeros_like(scores)
     squares[...] = jnp.zeros_like(squares)
+
+    def placed(shape, dim):
+        position = lax.broadcasted_iota(jnp.int32, shape, dim)
+        owner = jnp.full(shape, -1, jnp.int32)
+        source = jnp.full(shape, -1, jnp.int32)
+        start = 0
+        for d in range(doc_total):
+            end = start + lengths_ref[d]
+            inside = (position >= start) & (position < end)
+            owner = jnp.where(inside, d, owner)
+            source = jnp.where(inside, d * doc_span + position - start, source)
+            start = end
+        return owner, source
+
+    row_doc, row_source = placed((rows, 1), 0)
+    row_doc = jnp.maximum(row_doc, 0)
+    key_doc, _ = placed((1, rows), 1)
 
     def project(c, weight_dim):
         values = hid[:, cols(c)].astype(jnp.float32)
         squares[...] += jnp.sum(values * values, axis=-1, keepdims=True)
-        scaled = (values * gain_ref[:, cols(c)]).astype(jnp.bfloat16)
+        scaled = (values * enc_gain_ref[pl.ds(group, 1), cols(c)]).astype(jnp.bfloat16)
 
         def some(t):
             for u in range(per):
@@ -612,9 +719,14 @@
 
     @pl.when(group == 0)
     def _():
-        entry.wait()
+        origin = lax.broadcasted_iota(jnp.int32, (rows, x_ref.shape[0]), 1)
+        pick = (row_source == origin).astype(jnp.float32).astype(jnp.bfloat16)
 
         def first(c):
+            entry_copy(c).wait()
+            hid[:, cols(c)] = jnp.dot(
+                pick, entered[:, cols(c)], preferred_element_type=jnp.float32
+            ).astype(hid.dtype)
             weight_copy(c).wait()
             project(c, 1)
 
@@ -656,31 +768,48 @@
 
         each(chunks, complete)
 
+    def fetch(c):
+        query_copy(c).start()
+        key_copy(c).start()
+        close_copy(c).start()
+
+    each(chunks, fetch)
+
+    def fetch_head(i):
+        head_copy(i).start()
+
+    each(chunks * blocks, fetch_head)
+
+    def mixed_pair(queries, keys, values, allowed):
+        size = queries.shape[0]
+        first = lax.broadcasted_iota(jnp.int32, (size, 2 * HD), 1) < HD
+        both = jnp.concatenate(
+            [jnp.where(first, queries, 0.0), jnp.where(first, 0.0, queries)], 0
+        ).astype(jnp.bfloat16)
+        raw = lax.dot_general(
+            both, keys, (((1,), (1,)), ((), ())), preferred_element_type=jnp.float32
+        )
+        weights = jnp.where(allowed, jnp.exp(raw), 0.0)
+        shares = weights * (1.0 / jnp.sum(weights, axis=-1, keepdims=True))
+        mixed = jnp.dot(shares.astype(jnp.bfloat16), values, preferred_element_type=jnp.float32)
+        return jnp.where(first, mixed[:size], mixed[size:])
+
+    pairs = tile_columns // (2 * HD)
     scale = lax.rsqrt(squares[...] * (1.0 / width) + 1e-06)
-    pairs = tile_columns // (2 * HD)
-    allowed = row_doc_ref[...] == key_doc_ref[...]
+    allowed = row_doc == key_doc
     allowed = jnp.concatenate([allowed, allowed], 0)
-    first = lax.broadcasted_iota(jnp.int32, (rows, 2 * HD), 1) < HD
 
     def attend_tile(tile):
         for p in range(pairs):
             span = slice(p * 2 * HD, (p + 1) * 2 * HD)
-            queries = acc[tile, :, span] * scale
-            keys = (acc[per + tile, :, span] * scale).astype(jnp.bfloat16)
-            values = (acc[2 * per + tile, :, span] * scale).astype(jnp.bfloat16)
-            both = jnp.concatenate(
-                [jnp.where(first, queries, 0.0), jnp.where(first, 0.0, queries)], 0
-            ).astype(jnp.bfloat16)
-            scores = lax.dot_general(
-                both, keys, (((1,), (1,)), ((), ())), preferred_element_type=jnp.float32
+            mixed = mixed_pair(
+                acc[tile, :, span] * scale,
+                (acc[per + tile, :, span] * scale).astype(jnp.bfloat16),
+                (acc[2 * per + tile, :, span] * scale).astype(jnp.bfloat16),
+                allowed,
             )
-            weights = jnp.where(allowed, jnp.exp(scores), 0.0)
-            shares = weights * (1.0 / jnp.sum(weights, axis=-1, keepdims=True))
-            mixed = jnp.dot(shares.astype(jnp.bfloat16), values, preferred_element_type=jnp.float32)
             place = pl.multiple_of(tile * tile_columns + p * 2 * HD, 2 * HD)
-            mix[:, pl.ds(place, 2 * HD)] = jnp.where(first, mixed[:rows], mixed[rows:]).astype(
-                mix.dtype
-            )
+            mix[:, pl.ds(place, 2 * HD)] = mixed.astype(mix.dtype)
 
     each(per, attend_tile)
 
@@ -709,28 +838,145 @@
 
         each(chunks, finish)
 
-        def relay(c):
-            back(c).wait_recv()
-
-            @pl.when(group > 0)
-            def _():
-                back(c).start()
-
-            spread(c, own).start()
-
-        each(chunks, relay)
-
     @pl.when(group == GROUPS - 1)
     def _():
         def finish(c):
-            mem_ref[own, cols(c)] = total(c)
+            memory[own, cols(c)] = total(c)
             back(c).start()
             spread(c, own).start()
 
         each(chunks, finish)
 
+    def docid_rows(c):
+        return docid_ref[:, :, cols(c)].astype(jnp.float32).reshape(every, columns)
+
+    def ask(c, sums):
+        values = docid_rows(c)
+        scaled = (values * dec_gain_ref[0:1, cols(c)]).astype(jnp.bfloat16)
+        query_copy(c).wait()
+        query_acc[...] += lax.dot_general(
+            scaled, wqkv_v[c, 2], (((1,), (1,)), ((), ())), preferred_element_type=jnp.float32
+        )
+        return sums + jnp.sum(values * values, axis=-1, keepdims=True)
+
+    query_squares = lax.fori_loop(0, chunks, ask, jnp.zeros((every, 1), jnp.float32))
+    query_scale = lax.rsqrt(query_squares * (1.0 / width) + 1e-06)
+    squares[...] = jnp.zeros_like(squares)
+
+    def recall(c):
+        spread(c, other).wait_recv()
+        key_copy(c).wait()
+        values = memory[:, cols(c)].astype(jnp.float32)
+        squares[...] += jnp.sum(values * values, axis=-1, keepdims=True)
+        scaled = (values * enc_gain_ref[GROUPS : GROUPS + 1, cols(c)]).astype(jnp.bfloat16)
+        for j in range(2):
+            cross_acc[j] += lax.dot_general(
+                scaled, wqkv_v[c, j], (((1,), (1,)), ((), ())), preferred_element_type=jnp.float32
+            )
+
+    def relay(i):
+        @pl.when((i < chunks) & (group < GROUPS - 1))
+        def _():
+            back(i).wait_recv()
+
+            @pl.when(group > 0)
+            def _():
+                back(i).start()
+
+            spread(i, own).start()
+
+        @pl.when(i >= AHEAD)
+        def _():
+            recall(i - AHEAD)
+
+    each(chunks + AHEAD, relay)
+
+    memory_scale = lax.rsqrt(squares[...] * (1.0 / width) + 1e-06)
+    asking = lax.broadcasted_iota(jnp.int32, (every, 1), 0) // (every // doc_total)
+    visible = asking == key_doc
+    visible = jnp.concatenate([visible, visible], 0)
+    crossed = []
+    for p in range(pairs):
+        span = slice(p * 2 * HD, (p + 1) * 2 * HD)
+        crossed.append(
+            mixed_pair(
+                query_acc[:, span] * query_scale,
+                (cross_acc[0, :, span] * memory_scale).astype(jnp.bfloat16),
+                (cross_acc[1, :, span] * memory_scale).astype(jnp.bfloat16),
+                visible,
+            ).astype(jnp.bfloat16)
+        )
+    crossed = jnp.concatenate(crossed, 1)
+
+    def close(c):
+        close_copy(c).wait()
+        product = jnp.dot(crossed, wqkv_v[c, 3], preferred_element_type=jnp.float32)
+        terms[:, :, cols(c)] = product.reshape(share_count, share, columns).astype(terms.dtype)
+
+    each(chunks, close)
+    for k in range(1, count):
+        scatter(k, section).start()
+    summed = docid_ref[section].astype(jnp.float32) + terms[section].astype(jnp.float32)
+    for k in range(1, count):
+        scatter(k, source_of(k)).wait_recv()
+        summed = summed + landed[source_of(k)].astype(jnp.float32)
+    close_scale = lax.rsqrt(jnp.mean(summed * summed, axis=-1, keepdims=True) + 1e-06)
+    closing[section] = (summed * close_scale * dec_gain_ref[1:2, :]).astype(closing.dtype)
+    for k in range(1, count):
+        collect(k, section).start()
+
+    def arrive_head(i):
+        head_copy(i).wait()
+
+    each(chunks * blocks, arrive_head)
+    for k in range(1, count):
+        collect(k, source_of(k)).wait_recv()
+
+    def head(c):
+        final = closing[:, :, cols(c)].astype(jnp.float32).reshape(every, columns)
+        final = final.astype(jnp.bfloat16)
+        for b in range(blocks):
+            scores[b] += jnp.dot(final, wqkv_v[c, 4 + b], preferred_element_type=jnp.float32)
+
+    each(chunks, head)
+    summed_exp = jnp.zeros((every, 1), jnp.float32)
+    picked = jnp.zeros((every, 1), jnp.float32)
+    for b in range(blocks):
+        values = scores[b]
+        logits_ref[:, b * tile_columns : (b + 1) * tile_columns] = values.astype(logits_ref.dtype)
+        entry = lax.broadcasted_iota(jnp.int32, (every, tile_columns), 1)
+        entry = entry + (section * blocks + b) * tile_columns
+        summed_exp = summed_exp + jnp.sum(jnp.exp(values), axis=-1, keepdims=True)
+        picked = picked + jnp.sum(
+            jnp.where(entry == target_ref[...], values, 0.0), axis=-1, keepdims=True
+        )
+    place = lax.broadcasted_iota(jnp.int32, (every, 128), 1)
+    packed = jnp.where(place == 0, summed_exp, jnp.where(place == 1, picked, 0.0))
+    packed = jnp.concatenate([packed, jnp.zeros((128 - every, 128), jnp.float32)], 0)
+    stats[...] = packed.T[:8]
+    for k in range(1, count):
+        share_stats(k, section).start()
+    stats_landed[section] = stats[...]
+    for k in range(1, count):
+        share_stats(k, source_of(k)).wait_recv()
+    gathered = stats_landed[0]
+    for k in range(1, count):
+        gathered = gathered + stats_landed[k]
+    here = lax.broadcasted_iota(jnp.int32, (1, 128), 1) < every
+    token = jnp.log(jnp.where(here, gathered[0:1], 1.0)) - jnp.where(here, gathered[1:2], 0.0)
+    loss_ref[...] = jnp.broadcast_to(token, loss_ref.shape)
+    for k in range(1, rep_count):
+        share_loss(k, rep).start()
+    loss_landed[rep] = loss_ref[...]
+    for k in range(1, rep_count):
+        share_loss(k, lax.rem(rep + rep_count - k, rep_count)).wait_recv()
+    losses = loss_landed[0]
+    for k in range(1, rep_count):
+        losses = losses + loss_landed[k]
+    mean = jnp.sum(losses[0:1], axis=-1, keepdims=True) / (every * rep_count)
+    mean_ref[...] = jnp.broadcast_to(mean, mean_ref.shape)
+
     def drain(c):
-        spread(c, other).wait_recv()
         spread(c, own).wait_send()
         reduce(c).wait_send()
 
@@ -743,39 +989,139 @@
             back(c).wait_send()
 
     each(chunks, drain)
-
-
-def stream(rows, sent, number, x, gain, row_doc, key_doc, wqkv, wout):
+    for k in range(1, count):
+        scatter(k, section).wait_send()
+        collect(k, section).wait_send()
+        share_stats(k, section).wait_send()
+    for k in range(1, rep_count):
+        share_loss(k, rep).wait_send()
+
+
+def stream(sent, number, lengths, x, enc_gain, dec_gain, docid, targets, *weights):
     total_rows, width = x.shape
+    wqkv, wout, wcross, wclose, whead = weights
+    rows = total_rows // 2
     inner = wout.shape[0]
     tiles = 3 * (inner // WTILE)
+    columns = width // CHUNKS
+    share_count, share, _ = docid.shape
+    every = share_count * share
+    vocab = whead.shape[1]
     dma = pltpu.SemaphoreType.DMA
     vmem = pl.BlockSpec(memory_space=pltpu.VMEM)
+    smem = pl.BlockSpec(memory_space=pltpu.SMEM)
     anywhere = pl.BlockSpec(memory_space=pl.ANY)
-    return pl.pallas_call(
+    small = (8, 128)
+    bf16 = jnp.bfloat16
+    f32 = jnp.float32
+    reps = lax.axis_size("rep")
+    logits, loss, mean = pl.pallas_call(
         functools.partial(stream_kernel, sent),
-        out_shape=jax.ShapeDtypeStruct((total_rows, width), jnp.bfloat16),
-        in_specs=[anywhere, vmem, vmem, vmem, anywhere, anywhere],
-        out_specs=vmem,
+        out_shape=(
+            jax.ShapeDtypeStruct((every, vocab), bf16),
+            jax.ShapeDtypeStruct(small, f32),
+            jax.ShapeDtypeStruct(small, f32),
+        ),
+        in_specs=[smem, anywhere, vmem, vmem, vmem, vmem] + [anywhere] * 5,
+        out_specs=(vmem, vmem, vmem),
         scratch_shapes=[
-            pltpu.VMEM((CHUNKS, tiles, WTILE, width // CHUNKS), jnp.bfloat16),
-            pltpu.VMEM((CHUNKS, inner, width // CHUNKS), jnp.bfloat16),
-            pltpu.VMEM((rows, width), jnp.bfloat16),
-            pltpu.VMEM((rows, width), jnp.bfloat16),
-            pltpu.VMEM((sent // 2, width), jnp.bfloat16),
-            pltpu.VMEM((tiles, rows, WTILE), jnp.float32),
-            pltpu.VMEM((rows, 1), jnp.float32),
-            pltpu.VMEM((rows, inner), jnp.bfloat16),
-            dma((CHUNKS,)),
-            dma((CHUNKS,)),
-            dma,
+            pltpu.VMEM((CHUNKS, tiles, WTILE, columns), bf16),
+            pltpu.VMEM((CHUNKS, inner, columns), bf16),
+            pltpu.VMEM((total_rows, width), bf16),
+            pltpu.VMEM((rows, width), bf16),
+            pltpu.VMEM((rows, width), bf16),
+            pltpu.VMEM((sent // 2, width), bf16),
+            pltpu.VMEM((tiles, rows, WTILE), f32),
+            pltpu.VMEM((rows, 1), f32),
+            pltpu.VMEM((rows, inner), bf16),
+            pltpu.VMEM((rows, width), bf16),
+            pltpu.VMEM((2, rows, WTILE), f32),
+            pltpu.VMEM((every, WTILE), f32),
+            pltpu.VMEM(docid.shape, bf16),
+            pltpu.VMEM(docid.shape, bf16),
+            pltpu.VMEM(docid.shape, bf16),
+            pltpu.VMEM((vocab // WTILE, every, WTILE), f32),
+            pltpu.VMEM(small, f32),
+            pltpu.VMEM((share_count,) + small, f32),
+            pltpu.VMEM((reps,) + small, f32),
         ]
-        + [dma((CHUNKS,))] * 10,
+        + [dma((CHUNKS,))] * 16
+        + [dma((CHUNKS * (vocab // WTILE),))]
+        + [dma((share_count,))] * 6
+        + [dma((reps,))] * 2,
         compiler_params=pltpu.CompilerParams(
             collective_id=number, has_side_effects=True, vmem_limit_bytes=67043328
         ),
         name=f"stream_{sent}",
-    )(x, gain, row_doc[:rows, None], key_doc[None, :rows], wqkv.reshape(tiles, WTILE, width), wout)
+    )(
+        lengths,
+        x,
+        enc_gain,
+        dec_gain,
+        docid,
+        targets,
+        wqkv.reshape(tiles, WTILE, width),
+        wout,
+        wcross,
+        wclose,
+        whead,
+    )
+    return logits, loss[0, :every], mean[0, 0]
+
+
+def largest_kernel(limits, lengths_ref, out_ref, mine, landed, send, recv):
+    me = lax.axis_index("rep")
+    count = lax.axis_size("rep")
+    barrier = pltpu.get_barrier_semaphore()
+    for k in range(1, count):
+        pl.semaphore_signal(
+            barrier, inc=1, device_id={"rep": lax.rem(me + k, count)}, device_id_type=MESH
+        )
+    live = lengths_ref[0]
+    for d in range(1, lengths_ref.shape[0]):
+        live = live + lengths_ref[d]
+    mine[...] = jnp.full(mine.shape, live, jnp.int32).astype(jnp.float32)
+    pl.semaphore_wait(barrier, count - 1)
+
+    def share(k, slot):
+        return pltpu.make_async_remote_copy(
+            src_ref=mine,
+            dst_ref=landed.at[slot],
+            send_sem=send.at[k],
+            recv_sem=recv.at[k],
+            device_id={"rep": lax.rem(me + k, count)},
+            device_id_type=MESH,
+        )
+
+    for k in range(1, count):
+        share(k, me).start()
+    most = mine[...]
+    for k in range(1, count):
+        slot = lax.rem(me + count - k, count)
+        share(k, slot).wait_recv()
+        most = jnp.maximum(most, landed[slot])
+    choice = jnp.zeros(most.shape, jnp.float32)
+    for limit in limits:
+        choice = choice + jnp.where(most > limit, 1.0, 0.0)
+    out_ref[...] = choice.astype(jnp.int32)
+    for k in range(1, count):
+        share(k, me).wait_send()
+
+
+def branch_choice(limits, lengths):
+    count = lax.axis_size("rep")
+    dma = pltpu.SemaphoreType.DMA
+    small = (8, 128)
+    return pl.pallas_call(
+        functools.partial(largest_kernel, limits),
+        out_shape=jax.ShapeDtypeStruct(small, jnp.int32),
+        in_specs=[pl.BlockSpec(memory_space=pltpu.SMEM)],
+        out_specs=pl.BlockSpec(memory_space=pltpu.VMEM),
+        scratch_shapes=[pltpu.VMEM(small, jnp.float32), pltpu.VMEM((count,) + small, jnp.float32)]
+        + [dma((count,))] * 2,
+        compiler_params=pltpu.CompilerParams(collective_id=10, has_side_effects=True),
+        name="largest",
+    )(lengths)[0, 0]
 
 
 def butterfly(value, axis, combine):
@@ -884,7 +1230,7 @@
     )(value)
 
 
-def fast_shards(
+def large_shards(
     document_token_embedding,
     doc_lengths,
     docid_embed,
@@ -904,36 +1250,20 @@
     doc_span = row_count // doc_count
     all_rows = micro_count * row_count
     positions = jnp.arange(all_rows)
-    lengths = doc_lengths.reshape(-1)
-    live = (jnp.arange(doc_span)[None, :] < lengths[:, None]).reshape(-1)
-    ends = jnp.cumsum(lengths)
-    live_count = ends[-1]
-    starts = jnp.concatenate([jnp.zeros((1,), ends.dtype), ends[:-1]])
-    inside = (positions[:, None] >= starts[None, :]) & (positions[:, None] < ends[None, :])
-    docs = jnp.arange(lengths.shape[0])
-    row_doc = jnp.sum(jnp.where(inside, docs[None, :], 0), axis=1).astype(jnp.int32)
-    key_doc = jnp.where(positions < live_count, row_doc, -1).astype(jnp.int32)
-    source = jnp.sum(
-        jnp.where(inside, docs[None, :] * doc_span + positions[:, None] - starts[None, :], 0), axis=1
-    )
-    source = jnp.where(positions < live_count, source, -1)
-    pick = (source[:, None] == positions[None, :]).astype(jnp.bfloat16)
-    packed = jnp.dot(
-        pick,
+    row_doc = (positions // doc_span).astype(jnp.int32)
+    live = (jnp.arange(doc_span)[None, :] < doc_lengths.reshape(-1)[:, None]).reshape(-1)
+    key_doc = jnp.where(live, row_doc, -1).astype(jnp.int32)
+    gain = lax.dynamic_slice_in_dim(enc_gain, group_index, 1, 0)
+    hidden = encode(
+        all_rows,
+        all_rows,
+        2,
         document_token_embedding.reshape(all_rows, width),
-        preferred_element_type=jnp.float32,
-    ).astype(jnp.bfloat16)
-    largest = butterfly(live_count.astype(jnp.float32)[None], "rep", jnp.maximum)[0]
-    gain = lax.dynamic_slice_in_dim(enc_gain, group_index, 1, 0)
-    unit = all_rows // 2
-    sizes = [(unit, unit * 3 // 4), (unit, unit), (all_rows, all_rows)]
-    choice = jnp.sum(jnp.stack([(largest > sent).astype(jnp.int32) for _, sent in sizes[:-1]]))
-    branches = [
-        functools.partial(encode if rows > unit else stream, rows, sent, number)
-        for number, (rows, sent) in enumerate(sizes)
-    ]
-    hidden = lax.switch(
-        choice, branches, packed, gain, row_doc, key_doc, w_enc_qkv, w_enc_out
+        gain,
+        row_doc,
+        key_doc,
+        w_enc_qkv,
+        w_enc_out,
     )
     memory = norm_rows(hidden, enc_gain[GROUPS]).astype(jnp.bfloat16)
 
@@ -985,6 +1315,58 @@
     return (logits, token_loss.reshape(docid_targets.shape), mean_loss)
 
 
+def fast_shards(
+    document_token_embedding,
+    doc_lengths,
+    docid_embed,
+    docid_targets,
+    enc_gain,
+    dec_gain,
+    *weights,
+):
+    micro_count, row_count, width = document_token_embedding.shape
+    decoder_rows = docid_embed.shape[1]
+    sizes = (row_count * 3 // 4, row_count)
+    section_count = lax.axis_size("section")
+    lengths = doc_lengths.reshape(-1)
+    choice = branch_choice(sizes, lengths)
+
+    def streamed(sent, number):
+        def run():
+            logits, token_loss, mean_loss = stream(
+                sent,
+                number,
+                lengths,
+                document_token_embedding.reshape(micro_count * row_count, width),
+                enc_gain,
+                dec_gain,
+                docid_embed.reshape(section_count, -1, width),
+                docid_targets.reshape(-1, 1),
+                *weights,
+            )
+            return (
+                logits.reshape(micro_count, decoder_rows, -1),
+                token_loss.reshape(docid_targets.shape),
+                mean_loss,
+            )
+
+        return run
+
+    def large():
+        return large_shards(
+            document_token_embedding,
+            doc_lengths,
+            docid_embed,
+            docid_targets,
+            enc_gain,
+            dec_gain,
+            *weights,
+        )
+
+    branches = [streamed(sent, number) for number, sent in enumerate(sizes)] + [large]
+    return lax.switch(choice, branches)
+
+
 def solution(mesh):
     in_specs = (
         P("rep", None, None),

time: 219 us -> 182 us (0.83)
  matrix products: 29.3 us -> 0 us
  Pallas kernels: 158 us -> 172 us
  starting transfers between devices: 8.07 us -> 0 us
  other arithmetic: 8.03 us -> 0 us
  between operations: 5.9 us -> 1.29 us
    dot_general x8 -> x0, matrix products: 29.3 us -> none  [the longest x3 11.4 us: project(): jnp.einsum('rd,cd->rc', values, weight, preferred_element_type=jnp.float32)]
    pallas_call x3 -> x2, Pallas kernels: 158 us -> 172 us  [the longest x1 166 us: stream(): pl.pallas_call(functools.partial(stream_kernel, sent), out_shape=(jax.Sha...]
    ppermute x4 -> x0, starting transfers between devices: 8.07 us -> none  [from_partner(): return lax.ppermute(block, axis, route)]
    reduce_sum x4 -> x0, other arithmetic: 4.38 us -> none  [the longest x2 2.28 us: norm_rows(): scale = lax.rsqrt(jnp.mean(values * values, axis=-1, keepdims=True) + 1e-06)]
  transfers between devices with their start and end apart: 4 -> 0, of which waited for: 3 -> 0; matrix products, arithmetic and copies ran while one was open for 7% -> 0% of each run, Pallas kernels for 0% -> 0%
where the time goes in v1:
time: 182 us; the launch traced here: 181 us
  Pallas kernels  172 us (95%)
  local copies, waits for them, and re-layouts  8.07 us (4%)
    pallas_call x1, Pallas kernels, stream(): pl.pallas_call(functools.partial(stream_kernel, sent), out_shape=(jax.Sha...  166 us
    pallas_call x1, Pallas kernels, branch_choice(): pl.pallas_call(functools.partial(largest_kernel, limits), out_shape=jax.S...  5.93 us

profile of v1, /device:TPU:0, one launch (start us, length us, event | category | flops | bytes accessed | tf_op | source)
XLA Modules:
  0.0 181.3 jit_solution(11895309421029597133)
XLA Ops:
  0.6 1.3 reshape.253.lengths_ref
  1.9 5.9 %largest.1 = s32[8,128]{1,0:T(8,128)} custom-call(s32[8]{0:T(128)} %reshape.253.lengths_ref), custom_call_target="tpu_custom_call" | custom-call | tf_op jit(solution)/shard_map/largest/pallas_call | solution.py:1115
  7.8 1.2 slice.42
  9.7 169.9 %conditional.1 = (bf16[2,32,2048]{2,1,0:T(8,128)(2,1)}, f32[2,32]{1,0:T(2,128)}, f32[]{:T(128)}) conditional(s32[]{:T(128)} %bitcast.29, (bf16[2,128,4096]{2,1,0:T(8,128)(2,1)}, bf16[2,32,4096]{2,1,0:T(8,128)(2,1)}, s32[2,32]{1,0:T(2,128)}, bf16[3,1536,4096]{2,1,0:T(8,128)(2,1)}, s32[8]{0:T(128)}, /*index=5*/f32[5,4096]{1,0:T(8,128)}, ...), branch_computations={%region_0.0_spmd, %region_1.0_spmd, %region_2.9_spmd} | conditional | flops 3806726400 | bytes 57859068 | solution.py:1367
  9.7 1.4 reshape.254.target_ref
  11.1 165.9 %stream_96.1 = (bf16[64,2048]{1,0:T(8,128)(2,1)}, f32[8,128]{1,0:T(8,128)}, f32[8,128]{1,0:T(8,128)}) custom-call(s32[8]{0:T(128)} %get-tuple-element.66.lengths_ref, bf16[256,4096]{1,0:T(8,128)(2,1)} %bitcast.57, f32[5,4096]{1,0:T(8,128)} %get-tuple-element.68.enc_gain_ref, f32[2,4096]{1,0:T(2,128)} %get-tuple-element.69.dec_gain_ref, ...), custom_call_target="tpu_custom_call" | custom-call | tf_op jit(solution)/shard_map/cond/branch_0_fun/stream_96/pallas_call | solution.py:1018
  177.1 0.7 slice_reduce_fusion
  177.8 0.6 squeeze.5
  178.4 1.2 slice.30
  179.6 1.7 copy.47

commit v2 on v1

--- a/solution.py
+++ b/solution.py
@@ -12,7 +12,9 @@
 WTILE = 512
 PARTS = 4
 CHUNKS = 8
-AHEAD = 2
+AHEAD = 3
+HALVES = 2
+TAIL = 4
 MESH = pl.DeviceIdType.MESH
 
 
@@ -512,6 +514,9 @@
     query_acc,
     terms,
     landed,
+    partial,
+    crossed_over,
+    summed,
     closing,
     scores,
     stats,
@@ -534,8 +539,12 @@
     q_sem,
     c_sem,
     h_sem,
+    ys,
+    yr,
     ts,
     tr,
+    us,
+    ur,
     fs,
     fr,
     ss,
@@ -547,7 +556,8 @@
     half = sent // 2
     chunks, tiles, tile_columns, columns = wqkv_v.shape
     per = tiles // 3
-    doc_total = lengths_ref.shape[0]
+    micro_count, doc_count = lengths_ref.shape
+    doc_total = micro_count * doc_count
     doc_span = x_ref.shape[0] // doc_total
     share_count, share, _ = docid_ref.shape
     every = share_count * share
@@ -606,22 +616,31 @@
             device_id_type=MESH,
         )
 
-    def gather(c, block):
-        return remote(hid.at[block, cols(c)], hid.at[block, cols(c)], gs.at[c], gr.at[c], partner)
-
-    def reduce(c):
-        return remote(work.at[other, cols(c)], part.at[:, cols(c)], rs.at[c], rr.at[c], partner)
-
-    def hand(c):
-        return remote(hid.at[own, cols(c)], hid.at[own, cols(c)], zs.at[c], zr.at[c], ahead)
-
-    def back(c):
-        return remote(memory.at[own, cols(c)], memory.at[own, cols(c)], bs.at[c], br.at[c], behind)
-
-    def spread(c, block):
-        return remote(
-            memory.at[block, cols(c)], memory.at[block, cols(c)], ms.at[c], mr.at[c], partner
-        )
+    pieces = chunks * HALVES
+    piece = columns // HALVES
+
+    def span_of(i):
+        return pl.ds(pl.multiple_of(i * piece, piece), piece)
+
+    def gather(i, block):
+        place = hid.at[block, span_of(i)]
+        return remote(place, place, gs.at[i], gr.at[i], partner)
+
+    def reduce(i):
+        place = span_of(i)
+        return remote(work.at[other, place], part.at[:, place], rs.at[i], rr.at[i], partner)
+
+    def hand(i):
+        place = hid.at[own, span_of(i)]
+        return remote(place, place, zs.at[i], zr.at[i], ahead)
+
+    def back(i):
+        place = memory.at[own, span_of(i)]
+        return remote(place, place, bs.at[i], br.at[i], behind)
+
+    def spread(i, block):
+        place = memory.at[block, span_of(i)]
+        return remote(place, place, ms.at[i], mr.at[i], partner)
 
     def peer(k):
         return lax.rem(section + k, count)
@@ -629,11 +648,57 @@
     def source_of(k):
         return lax.rem(section + count - k, count)
 
-    def scatter(k, slot):
-        return remote(terms.at[peer(k)], landed.at[slot], ts.at[k], tr.at[k], peer(k))
-
-    def collect(k, slot):
-        return remote(closing.at[slot], closing.at[slot], fs.at[k], fr.at[k], peer(k))
+    stretch = width // TAIL
+    lanes = count // GROUPS
+    own_slot = lane * GROUPS + group
+
+    def tail_cols(t):
+        return pl.ds(pl.multiple_of(t * stretch, stretch), stretch)
+
+    def group_after(k):
+        return lax.rem(group + k, GROUPS)
+
+    def group_before(k):
+        return lax.rem(group + GROUPS - k, GROUPS)
+
+    def swap(t):
+        theirs = pl.ds((1 - lane) * GROUPS, GROUPS)
+        place = tail_cols(t)
+        return remote(
+            terms.at[theirs, :, place], landed.at[:, :, place], ys.at[t], yr.at[t], partner
+        )
+
+    def scatter(t, k):
+        place = tail_cols(t)
+        i = k * TAIL + t
+        return remote(
+            partial.at[group_after(k), :, place],
+            crossed_over.at[group, :, place],
+            ts.at[i],
+            tr.at[i],
+            group_after(k) * lanes + lane,
+        )
+
+    def scattered(t, k):
+        place = tail_cols(t)
+        i = k * TAIL + t
+        return remote(
+            partial.at[group, :, place],
+            crossed_over.at[group_before(k), :, place],
+            ts.at[i],
+            tr.at[i],
+            group_after(k) * lanes + lane,
+        )
+
+    def collect(t, k, slot):
+        place = closing.at[slot, :, tail_cols(t)]
+        i = k * TAIL + t
+        return remote(place, place, us.at[i], ur.at[i], group_after(k) * lanes + lane)
+
+    def across(t, member, side):
+        place = closing.at[side * GROUPS + member, :, tail_cols(t)]
+        i = member * TAIL + t
+        return remote(place, place, fs.at[i], fr.at[i], partner)
 
     def share_stats(k, slot):
         return remote(stats, stats_landed.at[slot], ss.at[k], sr.at[k], peer(k))
@@ -689,7 +754,7 @@
         source = jnp.full(shape, -1, jnp.int32)
         start = 0
         for d in range(doc_total):
-            end = start + lengths_ref[d]
+            end = start + lengths_ref[d // doc_count, d % doc_count]
             inside = (position >= start) & (position < end)
             owner = jnp.where(inside, d, owner)
             source = jnp.where(inside, d * doc_span + position - start, source)
@@ -699,6 +764,16 @@
     row_doc, row_source = placed((rows, 1), 0)
     row_doc = jnp.maximum(row_doc, 0)
     key_doc, _ = placed((1, rows), 1)
+
+    asked = target_ref.shape[1]
+    wanted = jnp.concatenate(
+        [jnp.broadcast_to(target_ref[m : m + 1, :], (asked, asked)) for m in range(micro_count)], 0
+    )
+    diagonal = lax.broadcasted_iota(jnp.int32, (every, asked), 0) % asked
+    diagonal = diagonal == lax.broadcasted_iota(jnp.int32, (every, asked), 1)
+    wanted = jnp.sum(
+        jnp.where(diagonal, wanted.astype(jnp.float32), 0.0), axis=-1, keepdims=True
+    )
 
     def project(c, weight_dim):
         values = hid[:, cols(c)].astype(jnp.float32)
@@ -743,8 +818,10 @@
                 whole = wqkv_v[c, j]
                 for a in range(2):
                     for b in range(2):
-                        piece = whole[a * side : (a + 1) * side, b * side : (b + 1) * side]
-                        wqkv_v[c, j, b * side : (b + 1) * side, a * side : (a + 1) * side] = piece.T
+                        quarter = whole[a * side : (a + 1) * side, b * side : (b + 1) * side]
+                        wqkv_v[c, j, b * side : (b + 1) * side, a * side : (a + 1) * side] = (
+                            quarter.T
+                        )
 
             each(tiles, block)
 
@@ -753,20 +830,22 @@
         def step(i):
             @pl.when(i < chunks)
             def _():
-                hand(i).wait_recv()
-                gather(i, own).start()
+                for u in range(HALVES):
+                    hand(i * HALVES + u).wait_recv()
+                    gather(i * HALVES + u, own).start()
 
             @pl.when(i >= AHEAD)
             def _():
-                gather(i - AHEAD, other).wait_recv()
+                for u in range(HALVES):
+                    gather((i - AHEAD) * HALVES + u, other).wait_recv()
                 project(i - AHEAD, 0)
 
         each(chunks + AHEAD, step)
 
-        def complete(c):
-            gather(c, own).wait_send()
-
-        each(chunks, complete)
+        def complete(i):
+            gather(i, own).wait_send()
+
+        each(pieces, complete)
 
     def fetch(c):
         query_copy(c).start()
@@ -818,34 +897,35 @@
         work[:, cols(c)] = jnp.dot(
             mix[...], wout_v[c], preferred_element_type=jnp.float32
         ).astype(work.dtype)
-        reduce(c).start()
+        for u in range(HALVES):
+            reduce(c * HALVES + u).start()
 
     each(chunks, output)
 
-    def total(c):
-        reduce(c).wait_recv()
+    def total(i):
+        reduce(i).wait_recv()
         return (
-            hid[own, cols(c)].astype(jnp.float32)
-            + work[own, cols(c)].astype(jnp.float32)
-            + part[:, cols(c)].astype(jnp.float32)
+            hid[own, span_of(i)].astype(jnp.float32)
+            + work[own, span_of(i)].astype(jnp.float32)
+            + part[:, span_of(i)].astype(jnp.float32)
         ).astype(hid.dtype)
 
     @pl.when(group < GROUPS - 1)
     def _():
-        def finish(c):
-            hid[own, cols(c)] = total(c)
-            hand(c).start()
-
-        each(chunks, finish)
+        def finish(i):
+            hid[own, span_of(i)] = total(i)
+            hand(i).start()
+
+        each(pieces, finish)
 
     @pl.when(group == GROUPS - 1)
     def _():
-        def finish(c):
-            memory[own, cols(c)] = total(c)
-            back(c).start()
-            spread(c, own).start()
-
-        each(chunks, finish)
+        def finish(i):
+            memory[own, span_of(i)] = total(i)
+            back(i).start()
+            spread(i, own).start()
+
+        each(pieces, finish)
 
     def docid_rows(c):
         return docid_ref[:, :, cols(c)].astype(jnp.float32).reshape(every, columns)
@@ -864,7 +944,8 @@
     squares[...] = jnp.zeros_like(squares)
 
     def recall(c):
-        spread(c, other).wait_recv()
+        for u in range(HALVES):
+            spread(c * HALVES + u, other).wait_recv()
         key_copy(c).wait()
         values = memory[:, cols(c)].astype(jnp.float32)
         squares[...] += jnp.sum(values * values, axis=-1, keepdims=True)
@@ -877,13 +958,14 @@
     def relay(i):
         @pl.when((i < chunks) & (group < GROUPS - 1))
         def _():
-            back(i).wait_recv()
-
-            @pl.when(group > 0)
-            def _():
-                back(i).start()
-
-            spread(i, own).start()
+            for u in range(HALVES):
+                back(i * HALVES + u).wait_recv()
+
+                @pl.when(group > 0)
+                def _():
+                    back(i * HALVES + u).start()
+
+                spread(i * HALVES + u, own).start()
 
         @pl.when(i >= AHEAD)
         def _():
@@ -908,47 +990,92 @@
         )
     crossed = jnp.concatenate(crossed, 1)
 
-    def close(c):
-        close_copy(c).wait()
-        product = jnp.dot(crossed, wqkv_v[c, 3], preferred_element_type=jnp.float32)
-        terms[:, :, cols(c)] = product.reshape(share_count, share, columns).astype(terms.dtype)
-
-    each(chunks, close)
-    for k in range(1, count):
-        scatter(k, section).start()
-    summed = docid_ref[section].astype(jnp.float32) + terms[section].astype(jnp.float32)
-    for k in range(1, count):
-        scatter(k, source_of(k)).wait_recv()
-        summed = summed + landed[source_of(k)].astype(jnp.float32)
-    close_scale = lax.rsqrt(jnp.mean(summed * summed, axis=-1, keepdims=True) + 1e-06)
-    closing[section] = (summed * close_scale * dec_gain_ref[1:2, :]).astype(closing.dtype)
-    for k in range(1, count):
-        collect(k, section).start()
+    ratio = chunks // TAIL
+
+    def close(t):
+        for u in range(ratio):
+            c = t * ratio + u
+            close_copy(c).wait()
+            product = jnp.dot(crossed, wqkv_v[c, 3], preferred_element_type=jnp.float32)
+            terms[:, :, cols(c)] = product.reshape(share_count, share, columns).astype(terms.dtype)
+        swap(t).start()
+
+    each(TAIL, close)
+    mine = pl.ds(lane * GROUPS, GROUPS)
+
+    def halfway(t):
+        swap(t).wait_recv()
+        both = terms[mine, :, tail_cols(t)].astype(jnp.float32)
+        both = both + landed[:, :, tail_cols(t)].astype(jnp.float32)
+        partial[:, :, tail_cols(t)] = both.astype(partial.dtype)
+        for m in range(1, GROUPS):
+            scatter(t, m).start()
+
+    each(TAIL, halfway)
+
+    def finished(t, squares_so_far):
+        place = tail_cols(t)
+        value = docid_ref[own_slot, :, place].astype(jnp.float32)
+        value = value + partial[group, :, place].astype(jnp.float32)
+        for m in range(1, GROUPS):
+            scattered(t, m).wait_recv()
+            value = value + crossed_over[group_before(m), :, place].astype(jnp.float32)
+        summed[:, place] = value
+        return squares_so_far + jnp.sum(value * value, axis=-1, keepdims=True)
+
+    close_squares = lax.fori_loop(0, TAIL, finished, jnp.zeros((share, 1), jnp.float32))
+    close_scale = lax.rsqrt(close_squares * (1.0 / width) + 1e-06)
+
+    def publish(t):
+        place = tail_cols(t)
+        value = summed[:, place] * close_scale * dec_gain_ref[1:2, place]
+        closing[own_slot, :, place] = value.astype(closing.dtype)
+        for m in range(1, GROUPS):
+            collect(t, m, own_slot).start()
+        across(t, group, lane).start()
+
+    each(TAIL, publish)
 
     def arrive_head(i):
         head_copy(i).wait()
 
     each(chunks * blocks, arrive_head)
-    for k in range(1, count):
-        collect(k, source_of(k)).wait_recv()
-
-    def head(c):
-        final = closing[:, :, cols(c)].astype(jnp.float32).reshape(every, columns)
-        final = final.astype(jnp.bfloat16)
-        for b in range(blocks):
-            scores[b] += jnp.dot(final, wqkv_v[c, 4 + b], preferred_element_type=jnp.float32)
-
-    each(chunks, head)
+
+    def forward(t):
+        for m in range(1, GROUPS):
+            member = group_before(m)
+            collect(t, m, lane * GROUPS + member).wait_recv()
+            across(t, member, lane).start()
+
+    def head(t):
+        for m in range(GROUPS):
+            across(t, m, 1 - lane).wait_recv()
+        for u in range(ratio):
+            c = t * ratio + u
+            final = closing[:, :, cols(c)].astype(jnp.float32).reshape(every, columns)
+            final = final.astype(jnp.bfloat16)
+            for b in range(blocks):
+                scores[b] += jnp.dot(final, wqkv_v[c, 4 + b], preferred_element_type=jnp.float32)
+
+    def spread_rows(t):
+        @pl.when(t < TAIL)
+        def _():
+            forward(t)
+
+        @pl.when(t >= 1)
+        def _():
+            head(t - 1)
+
+    each(TAIL + 1, spread_rows)
     summed_exp = jnp.zeros((every, 1), jnp.float32)
     picked = jnp.zeros((every, 1), jnp.float32)
     for b in range(blocks):
         values = scores[b]
-        logits_ref[:, b * tile_columns : (b + 1) * tile_columns] = values.astype(logits_ref.dtype)
         entry = lax.broadcasted_iota(jnp.int32, (every, tile_columns), 1)
-        entry = entry + (section * blocks + b) * tile_columns
+        entry = (entry + (section * blocks + b) * tile_columns).astype(jnp.float32)
         summed_exp = summed_exp + jnp.sum(jnp.exp(values), axis=-1, keepdims=True)
         picked = picked + jnp.sum(
-            jnp.where(entry == target_ref[...], values, 0.0), axis=-1, keepdims=True
+            jnp.where(entry == wanted, values, 0.0), axis=-1, keepdims=True
         )
     place = lax.broadcasted_iota(jnp.int32, (every, 128), 1)
     packed = jnp.where(place == 0, summed_exp, jnp.where(place == 1, picked, 0.0))
@@ -957,6 +1084,10 @@
     for k in range(1, count):
         share_stats(k, section).start()
     stats_landed[section] = stats[...]
+    for b in range(blocks):
+        logits_ref[:, b * tile_columns : (b + 1) * tile_columns] = scores[b].astype(
+            logits_ref.dtype
+        )
     for k in range(1, count):
         share_stats(k, source_of(k)).wait_recv()
     gathered = stats_landed[0]
@@ -976,22 +1107,30 @@
     mean = jnp.sum(losses[0:1], axis=-1, keepdims=True) / (every * rep_count)
     mean_ref[...] = jnp.broadcast_to(mean, mean_ref.shape)
 
-    def drain(c):
-        spread(c, own).wait_send()
-        reduce(c).wait_send()
+    def drain(i):
+        spread(i, own).wait_send()
+        reduce(i).wait_send()
 
         @pl.when(group < GROUPS - 1)
         def _():
-            hand(c).wait_send()
+            hand(i).wait_send()
 
         @pl.when(group > 0)
         def _():
-            back(c).wait_send()
-
-    each(chunks, drain)
-    for k in range(1, count):
-        scatter(k, section).wait_send()
-        collect(k, section).wait_send()
+            back(i).wait_send()
+
+    each(pieces, drain)
+
+    def drain_tail(t):
+        swap(t).wait_send()
+        for m in range(1, GROUPS):
+            scatter(t, m).wait_send()
+            collect(t, m, own_slot).wait_send()
+        for m in range(GROUPS):
+            across(t, m, lane).wait_send()
+
+    each(TAIL, drain_tail)
+    for k in range(1, count):
         share_stats(k, section).wait_send()
     for k in range(1, rep_count):
         share_loss(k, rep).wait_send()
@@ -1038,16 +1177,23 @@
             pltpu.VMEM((2, rows, WTILE), f32),
             pltpu.VMEM((every, WTILE), f32),
             pltpu.VMEM(docid.shape, bf16),
-            pltpu.VMEM(docid.shape, bf16),
+            pltpu.VMEM((GROUPS,) + docid.shape[1:], bf16),
+            pltpu.VMEM((GROUPS,) + docid.shape[1:], bf16),
+            pltpu.VMEM((GROUPS,) + docid.shape[1:], bf16),
+            pltpu.VMEM(docid.shape[1:], f32),
             pltpu.VMEM(docid.shape, bf16),
             pltpu.VMEM((vocab // WTILE, every, WTILE), f32),
             pltpu.VMEM(small, f32),
             pltpu.VMEM((share_count,) + small, f32),
             pltpu.VMEM((reps,) + small, f32),
         ]
-        + [dma((CHUNKS,))] * 16
+        + [dma((CHUNKS,))] * 3
+        + [dma((CHUNKS * HALVES,))] * 10
+        + [dma((CHUNKS,))] * 3
         + [dma((CHUNKS * (vocab // WTILE),))]
-        + [dma((share_count,))] * 6
+        + [dma((TAIL,))] * 2
+        + [dma((GROUPS * TAIL,))] * 6
+        + [dma((share_count,))] * 2
         + [dma((reps,))] * 2,
         compiler_params=pltpu.CompilerParams(
             collective_id=number, has_side_effects=True, vmem_limit_bytes=67043328
@@ -1077,9 +1223,10 @@
         pl.semaphore_signal(
             barrier, inc=1, device_id={"rep": lax.rem(me + k, count)}, device_id_type=MESH
         )
-    live = lengths_ref[0]
-    for d in range(1, lengths_ref.shape[0]):
-        live = live + lengths_ref[d]
+    live = 0
+    for m in range(lengths_ref.shape[0]):
+        for d in range(lengths_ref.shape[1]):
+            live = live + lengths_ref[m, d]
     mine[...] = jnp.full(mine.shape, live, jnp.int32).astype(jnp.float32)
     pl.semaphore_wait(barrier, count - 1)
 
@@ -1103,7 +1250,7 @@
     choice = jnp.zeros(most.shape, jnp.float32)
     for limit in limits:
         choice = choice + jnp.where(most > limit, 1.0, 0.0)
-    out_ref[...] = choice.astype(jnp.int32)
+    out_ref[0, 0] = jnp.max(choice).astype(jnp.int32)
     for k in range(1, count):
         share(k, me).wait_send()
 
@@ -1114,9 +1261,9 @@
     small = (8, 128)
     return pl.pallas_call(
         functools.partial(largest_kernel, limits),
-        out_shape=jax.ShapeDtypeStruct(small, jnp.int32),
+        out_shape=jax.ShapeDtypeStruct((1, 1), jnp.int32),
         in_specs=[pl.BlockSpec(memory_space=pltpu.SMEM)],
-        out_specs=pl.BlockSpec(memory_space=pltpu.VMEM),
+        out_specs=pl.BlockSpec(memory_space=pltpu.SMEM),
         scratch_shapes=[pltpu.VMEM(small, jnp.float32), pltpu.VMEM((count,) + small, jnp.float32)]
         + [dma((count,))] * 2,
         compiler_params=pltpu.CompilerParams(collective_id=10, has_side_effects=True),
@@ -1328,20 +1475,19 @@
     decoder_rows = docid_embed.shape[1]
     sizes = (row_count * 3 // 4, row_count)
     section_count = lax.axis_size("section")
-    lengths = doc_lengths.reshape(-1)
-    choice = branch_choice(sizes, lengths)
+    choice = branch_choice(sizes, doc_lengths)
 
     def streamed(sent, number):
         def run():
             logits, token_loss, mean_loss = stream(
                 sent,
                 number,
-                lengths,
+                doc_lengths,
                 document_token_embedding.reshape(micro_count * row_count, width),
                 enc_gain,
                 dec_gain,
                 docid_embed.reshape(section_count, -1, width),
-                docid_targets.reshape(-1, 1),
+                docid_targets,
                 *weights,
             )
             return (

time: 182 us -> 167 us (0.918)
  Pallas kernels: 172 us -> 161 us
  local copies, waits for them, and re-layouts: 8.07 us -> 4.2 us
    pallas_call x1, Pallas kernels: 166 us -> 155 us  [stream(): pl.pallas_call(functools.partial(stream_kernel, sent), out_shape=(jax.Sha...]
    reshape x2 -> x0, local copies, waits for them, and re-layouts: 2.68 us -> none  [the longest x1 1.4 us: run(): docid_targets.reshape(-1, 1)]
where the time goes in v2:
time: 167 us; the launch traced here: 166 us
  Pallas kernels  161 us (96%)
  local copies, waits for them, and re-layouts  4.2 us (3%)
    pallas_call x1, Pallas kernels, stream(): pl.pallas_call(functools.partial(stream_kernel, sent), out_shape=(jax.Sha...  155 us
    pallas_call x1, Pallas kernels, branch_choice(): pl.pallas_call(functools.partial(largest_kernel, limits), out_shape=jax.S...  6 us

profile of v2, /device:TPU:0, one launch (start us, length us, event | category | flops | bytes accessed | tf_op | source)
XLA Modules:
  0.0 166.5 jit_solution(2696088833954011628)
XLA Ops:
  0.6 6.0 %largest.1 = s32[1,1]{1,0:T(1,128)} custom-call(s32[2,4]{1,0:T(2,128)} %lengths_ref.1), custom_call_target="tpu_custom_call" | custom-call | tf_op jit(solution)/shard_map/largest/pallas_call | solution.py:1262
  7.3 157.5 %conditional.1 = (bf16[2,32,2048]{2,1,0:T(8,128)(2,1)}, f32[2,32]{1,0:T(2,128)}, f32[]{:T(128)}) conditional(s32[]{:T(128)} %bitcast.29, (bf16[2,128,4096]{2,1,0:T(8,128)(2,1)}, bf16[2,32,4096]{2,1,0:T(8,128)(2,1)}, bf16[3,1536,4096]{2,1,0:T(8,128)(2,1)}, s32[2,4]{1,0:T(2,128)}, f32[5,4096]{1,0:T(8,128)}, ...), branch_computations={%region_0.0_spmd, %region_1.0_spmd, %region_2.9_spmd} | conditional | flops 3806726400 | bytes 57859068 | solution.py:1513
  7.3 155.0 %stream_96.1 = (bf16[64,2048]{1,0:T(8,128)(2,1)}, f32[8,128]{1,0:T(8,128)}, f32[8,128]{1,0:T(8,128)}) custom-call(s32[2,4]{1,0:T(2,128)} %get-tuple-element.66.lengths_ref, bf16[256,4096]{1,0:T(8,128)(2,1)} %bitcast.57, f32[5,4096]{1,0:T(8,128)} %get-tuple-element.68.enc_gain_ref, f32[2,4096]{1,0:T(2,128)} %get-tuple-element.69.dec_gain_ref, ...), custom_call_target="tpu_custom_call" | custom-call | tf_op jit(solution)/shard_map/cond/branch_0_fun/stream_96/pallas_call | solution.py:1157
  162.3 0.7 slice_reduce_fusion
  163.0 0.6 squeeze.5
  163.6 1.2 slice.28
  164.8 1.7 %copy.43 = bf16[2,32,2048]{2,1,0:T(8,128)(2,1)} copy(bf16[2,32,2048]{2,1,0:T(8,128)(2,1)} %get-tuple-element.135) | data formatting | bytes 524288

commit v3 on v2

--- a/solution.py
+++ b/solution.py
@@ -498,7 +498,7 @@
     wclose_ref,
     whead_ref,
     logits_ref,
-    loss_ref,
+    token_ref,
     mean_ref,
     wqkv_v,
     wout_v,
@@ -521,6 +521,7 @@
     scores,
     stats,
     stats_landed,
+    loss_ref,
     loss_landed,
     w_sem,
     o_sem,
@@ -780,17 +781,13 @@
         squares[...] += jnp.sum(values * values, axis=-1, keepdims=True)
         scaled = (values * enc_gain_ref[pl.ds(group, 1), cols(c)]).astype(jnp.bfloat16)
 
-        def some(t):
-            for u in range(per):
-                j = t * per + u
-                acc[j] += lax.dot_general(
-                    scaled,
-                    wqkv_v[c, j],
-                    (((1,), (weight_dim,)), ((), ())),
-                    preferred_element_type=jnp.float32,
-                )
-
-        each(3, some)
+        for j in range(tiles):
+            acc[j] += lax.dot_general(
+                scaled,
+                wqkv_v[c, j],
+                (((1,), (weight_dim,)), ((), ())),
+                preferred_element_type=jnp.float32,
+            )
 
     @pl.when(group == 0)
     def _():
@@ -859,9 +856,11 @@
 
     each(chunks * blocks, fetch_head)
 
-    def mixed_pair(queries, keys, values, allowed):
-        size = queries.shape[0]
-        first = lax.broadcasted_iota(jnp.int32, (size, 2 * HD), 1) < HD
+    def halves(size):
+        return lax.broadcasted_iota(jnp.int32, (size, 2 * HD), 1) < HD
+
+    def share_keys(queries, keys, allowed):
+        first = halves(queries.shape[0])
         both = jnp.concatenate(
             [jnp.where(first, queries, 0.0), jnp.where(first, 0.0, queries)], 0
         ).astype(jnp.bfloat16)
@@ -870,27 +869,29 @@
         )
         weights = jnp.where(allowed, jnp.exp(raw), 0.0)
         shares = weights * (1.0 / jnp.sum(weights, axis=-1, keepdims=True))
-        mixed = jnp.dot(shares.astype(jnp.bfloat16), values, preferred_element_type=jnp.float32)
-        return jnp.where(first, mixed[:size], mixed[size:])
+        return shares.astype(jnp.bfloat16)
+
+    def mix_values(shares, values):
+        size = shares.shape[0] // 2
+        mixed = jnp.dot(shares, values, preferred_element_type=jnp.float32)
+        return jnp.where(halves(size), mixed[:size], mixed[size:])
 
     pairs = tile_columns // (2 * HD)
     scale = lax.rsqrt(squares[...] * (1.0 / width) + 1e-06)
     allowed = row_doc == key_doc
     allowed = jnp.concatenate([allowed, allowed], 0)
 
-    def attend_tile(tile):
-        for p in range(pairs):
-            span = slice(p * 2 * HD, (p + 1) * 2 * HD)
-            mixed = mixed_pair(
-                acc[tile, :, span] * scale,
-                (acc[per + tile, :, span] * scale).astype(jnp.bfloat16),
-                (acc[2 * per + tile, :, span] * scale).astype(jnp.bfloat16),
-                allowed,
-            )
-            place = pl.multiple_of(tile * tile_columns + p * 2 * HD, 2 * HD)
-            mix[:, pl.ds(place, 2 * HD)] = mixed.astype(mix.dtype)
-
-    each(per, attend_tile)
+    def pair_of(member, p):
+        at = slice(p % pairs * 2 * HD, (p % pairs + 1) * 2 * HD)
+        return acc[member * per + p // pairs, :, at] * scale
+
+    everyone = range(per * pairs)
+    shared = [
+        share_keys(pair_of(0, p), pair_of(1, p).astype(jnp.bfloat16), allowed) for p in everyone
+    ]
+    for p in everyone:
+        mixed = mix_values(shared[p], pair_of(2, p).astype(jnp.bfloat16))
+        mix[:, p * 2 * HD : (p + 1) * 2 * HD] = mixed.astype(mix.dtype)
 
     def output(c):
         out_copy(c).wait()
@@ -977,17 +978,20 @@
     asking = lax.broadcasted_iota(jnp.int32, (every, 1), 0) // (every // doc_total)
     visible = asking == key_doc
     visible = jnp.concatenate([visible, visible], 0)
-    crossed = []
-    for p in range(pairs):
-        span = slice(p * 2 * HD, (p + 1) * 2 * HD)
-        crossed.append(
-            mixed_pair(
-                query_acc[:, span] * query_scale,
-                (cross_acc[0, :, span] * memory_scale).astype(jnp.bfloat16),
-                (cross_acc[1, :, span] * memory_scale).astype(jnp.bfloat16),
-                visible,
-            ).astype(jnp.bfloat16)
-        )
+    spans = [slice(p * 2 * HD, (p + 1) * 2 * HD) for p in range(pairs)]
+    shared = [
+        share_keys(
+            query_acc[:, at] * query_scale,
+            (cross_acc[0, :, at] * memory_scale).astype(jnp.bfloat16),
+            visible,
+        )
+        for at in spans
+    ]
+    crossed = [
+        mix_values(shared[p], (cross_acc[1, :, spans[p]] * memory_scale).astype(jnp.bfloat16))
+        for p in range(pairs)
+    ]
+    crossed = [value.astype(jnp.bfloat16) for value in crossed]
     crossed = jnp.concatenate(crossed, 1)
 
     ratio = chunks // TAIL
@@ -1085,9 +1089,10 @@
         share_stats(k, section).start()
     stats_landed[section] = stats[...]
     for b in range(blocks):
-        logits_ref[:, b * tile_columns : (b + 1) * tile_columns] = scores[b].astype(
-            logits_ref.dtype
-        )
+        for m in range(micro_count):
+            logits_ref[m, :, b * tile_columns : (b + 1) * tile_columns] = scores[
+                b, m * asked : (m + 1) * asked
+            ].astype(logits_ref.dtype)
     for k in range(1, count):
         share_stats(k, source_of(k)).wait_recv()
     gathered = stats_landed[0]
@@ -1099,6 +1104,8 @@
     for k in range(1, rep_count):
         share_loss(k, rep).start()
     loss_landed[rep] = loss_ref[...]
+    for m in range(micro_count):
+        token_ref[m : m + 1, :] = token[:, m * asked : (m + 1) * asked]
     for k in range(1, rep_count):
         share_loss(k, lax.rem(rep + rep_count - k, rep_count)).wait_recv()
     losses = loss_landed[0]
@@ -1154,12 +1161,12 @@
     bf16 = jnp.bfloat16
     f32 = jnp.float32
     reps = lax.axis_size("rep")
-    logits, loss, mean = pl.pallas_call(
+    logits, token_loss, mean = pl.pallas_call(
         functools.partial(stream_kernel, sent),
         out_shape=(
-            jax.ShapeDtypeStruct((every, vocab), bf16),
-            jax.ShapeDtypeStruct(small, f32),
-            jax.ShapeDtypeStruct(small, f32),
+            jax.ShapeDtypeStruct(targets.shape + (vocab,), bf16),
+            jax.ShapeDtypeStruct(targets.shape, f32),
+            jax.ShapeDtypeStruct((1, 1), f32),
         ),
         in_specs=[smem, anywhere, vmem, vmem, vmem, vmem] + [anywhere] * 5,
         out_specs=(vmem, vmem, vmem),
@@ -1185,6 +1192,7 @@
             pltpu.VMEM((vocab // WTILE, every, WTILE), f32),
             pltpu.VMEM(small, f32),
             pltpu.VMEM((share_count,) + small, f32),
+            pltpu.VMEM(small, f32),
             pltpu.VMEM((reps,) + small, f32),
         ]
         + [dma((CHUNKS,))] * 3
@@ -1212,7 +1220,7 @@
         wclose,
         whead,
     )
-    return logits, loss[0, :every], mean[0, 0]
+    return logits, token_loss, mean[0, 0]
 
 
 def largest_kernel(limits, lengths_ref, out_ref, mine, landed, send, recv):
@@ -1472,14 +1480,13 @@
     *weights,
 ):
     micro_count, row_count, width = document_token_embedding.shape
-    decoder_rows = docid_embed.shape[1]
     sizes = (row_count * 3 // 4, row_count)
     section_count = lax.axis_size("section")
     choice = branch_choice(sizes, doc_lengths)
 
     def streamed(sent, number):
         def run():
-            logits, token_loss, mean_loss = stream(
+            return stream(
                 sent,
                 number,
                 doc_lengths,
@@ -1490,12 +1497,6 @@
                 docid_targets,
                 *weights,
             )
-            return (
-                logits.reshape(micro_count, decoder_rows, -1),
-                token_loss.reshape(docid_targets.shape),
-                mean_loss,
-            )
-
         return run
 
     def large():

time: 167 us -> 151 us (0.904)
  Pallas kernels: 161 us -> 144 us
  between operations: 1.26 us -> 3.03 us
    pallas_call x1, Pallas kernels: 155 us -> 138 us  [stream(): pl.pallas_call(functools.partial(stream_kernel, sent), out_shape=(jax.Sha...]
    slice x2 -> x0, local copies, waits for them, and re-layouts: 1.88 us -> none  [stream(): return (logits, loss[0, :every], mean[0, 0])]
where the time goes in v3:
time: 151 us
  Pallas kernels  144 us (95%)
  between operations  3.03 us (2%)
  local copies, waits for them, and re-layouts  2.91 us (2%)
    pallas_call x1, Pallas kernels, stream(): pl.pallas_call(functools.partial(stream_kernel, sent), out_shape=(jax.Sha...  138 us
    pallas_call x1, Pallas kernels, branch_choice(): pl.pallas_call(functools.partial(largest_kernel, limits), out_shape=jax.S...  6 us

profile of v3, /device:TPU:0, one launch (start us, length us, event | category | flops | bytes accessed | tf_op | source)
XLA Modules:
  0.0 150.6 jit_solution(18273558393741129403)
XLA Ops:
  0.6 6.0 %largest.1 = s32[1,1]{1,0:T(1,128)} custom-call(s32[2,4]{1,0:T(2,128)} %lengths_ref.1), custom_call_target="tpu_custom_call" | custom-call | tf_op jit(solution)/shard_map/largest/pallas_call | solution.py:1270
  7.3 138.7 %conditional.1 = (bf16[2,32,2048]{2,1,0:T(8,128)(2,1)}, f32[2,32]{1,0:T(2,128)}, f32[]{:T(128)}) conditional(s32[]{:T(128)} %bitcast.27, (bf16[2,128,4096]{2,1,0:T(8,128)(2,1)}, bf16[2,32,4096]{2,1,0:T(8,128)(2,1)}, bf16[3,1536,4096]{2,1,0:T(8,128)(2,1)}, s32[2,4]{1,0:T(2,128)}, f32[5,4096]{1,0:T(8,128)}, ...), branch_computations={%region_0.0_spmd, %region_1.0_spmd, %region_2.9_spmd} | conditional | flops 3806726400 | bytes 57859068 | solution.py:1514
  7.3 138.5 %stream_96.1 = (bf16[2,32,2048]{2,1,0:T(8,128)(2,1)}, f32[2,32]{1,0:T(2,128)}, f32[1,1]{1,0:T(1,128)}) custom-call(s32[2,4]{1,0:T(2,128)} %get-tuple-element.66.lengths_ref, bf16[256,4096]{1,0:T(8,128)(2,1)} %bitcast.55, f32[5,4096]{1,0:T(8,128)} %get-tuple-element.68.enc_gain_ref, f32[2,4096]{1,0:T(2,128)} %get-tuple-element.69.dec_gain_ref, ...), custom_call_target="tpu_custom_call" | custom-call | tf_op jit(solution)/shard_map/cond/branch_0_fun/stream_96/pallas_call | solution.py:1164
  146.0 1.7 %copy.39 = bf16[2,32,2048]{2,1,0:T(8,128)(2,1)} copy(bf16[2,32,2048]{2,1,0:T(8,128)(2,1)} %get-tuple-element.133) | data formatting | bytes 524288
  147.7 1.2 copy.40
